TPU v7x, 128 devices: a whole 4x4x4 slice. The times are simulated.
128 devices in a mesh: row: 8 (over z, y_lo), col: 4 (over x), chan: 4 (over y_hi, core).
Axes of the slice: x: 4, y: 4 (y_hi: 2, y_lo: 2; y = y_hi * 2 + y_lo), z: 4, core: 2. Of those that a mesh axis runs over, the one named last changes fastest.
Arguments:
- image_gen: float32 [3, 2048, 4096], P(None, ('row', 'chan'), 'col'), may hold values from -3 to 3
- image_ref: float32 [3, 2048, 4096], P(None, ('row', 'chan'), 'col'), may hold values from -1 to 1
- kernel_one: bfloat16 [3, 3, 48, 64], replicated, may hold values from -0.3125 to 0.3125
- bias_one: float32 [64], replicated, may hold values from -1.5 to 1.5
- kernel_two: bfloat16 [5, 5, 64, 192], replicated, may hold values from -0.15625 to 0.15625
- bias_two: float32 [192], replicated, may hold values from -1.5 to 1.5
- kernel_three: bfloat16 [3, 3, 192, 384], P(None, None, None, 'chan'), may hold values from -0.15625 to 0.15625
- bias_three: float32 [384], replicated, may hold values from -1.5 to 1.5
- lin_first: float32 [64], replicated, may hold values from 0.1 to 1
- lin_second: float32 [192], replicated, may hold values from 0.1 to 1
- lin_third: float32 [384], replicated, may hold values from 0.1 to 1
Outputs:
- image_grad: float32 [3, 2048, 4096], P(None, ('row', 'chan'), 'col')
- loss: float32 [], replicated
All inputs are finite; a program needn't handle non-finite values.
Results may differ from a plain program's by a relative error of at most 0.0086.
Values may be sent and summed in bfloat16 or wider, within the bound.
A program may use at most 128 MiB of HBM per device.

v0:
```python
import functools

import jax
import jax.numpy as jnp
from jax import lax
from jax.experimental import pallas as pl
from jax.experimental.pallas import tpu as pltpu
from jax.sharding import PartitionSpec as P

OFFSETS = (-0.03, -0.088, -0.188)
SPREADS = (0.458, 0.448, 0.45)
EPSILON = 1e-06
BF = jnp.bfloat16
F32 = jnp.float32
DIRS = ((-1, 0), (1, 0), (0, -1), (0, 1), (-1, -1), (-1, 1), (1, -1), (1, 1))
UP, DOWN, LEFT, RIGHT, UL, UR, DL, DR = range(8)
OPP = (1, 0, 3, 2, 7, 6, 5, 4)
STAGES = 8


def roll(x, shift):
    return pltpu.roll(x, shift % 128, 1)


def dot(a, b):
    return jnp.dot(a, b, preferred_element_type=F32)


def lanes(shape):
    return lax.broadcasted_iota(jnp.int32, shape, 1)


def shifted(x, e):
    low = lanes(x.shape) < 64
    if e == 1:
        return jnp.where(low, roll(x, 64), roll(x, 63))
    if e == -1:
        return jnp.where(low, roll(x, 65), roll(x, 64))
    return roll(x, -e // 2)


def kernel(
    img0, img1, wb1, w2t, w2n, w3s, wb1b, b1, b2, b3, l1, l2, l3,
    grad, loss,
    sel, pf, ef, tmp, lw, ew, x1, f1, sl1, pool1, x2, f2, sl2, keep, pool2, x3,
    f3, sl3, d3, x3d, w3t, w3n, dp2, d2, x4, yb, xh, yh, d1, x5, bf,
    cb1, cb2, cb3, cl1, cl2, cl3, la, lsa, lsb, lsc,
    su0, sd0, se0, seu, sed, ru0, rd0, rl0, rr0, rc0,
    se1, hs1, se2, hs2, ru2, rd2, se3, hs3, ru3, rd3, se4, hs4, se5, hs5, ru5, rd5,
    send_sem, recv_sem, wsend, wrecv, lsend, lrecv,
):
    n_row, n_col, n_chan = lax.axis_size("row"), lax.axis_size("col"), lax.axis_size("chan")
    i_row, i_col, i_chan = lax.axis_index("row"), lax.axis_index("col"), lax.axis_index("chan")
    tile = i_row * n_chan + i_chan
    n_tile = n_row * n_chan

    def place(step_t, step_c):
        other = tile + step_t
        return {"row": other // n_chan, "chan": other % n_chan, "col": i_col + step_c}

    def exists(step_t, step_c):
        ok = None
        for step, at, count in ((step_t, tile, n_tile), (step_c, i_col, n_col)):
            if step < 0:
                term = at > 0
            elif step > 0:
                term = at < count - 1
            else:
                continue
            ok = term if ok is None else jnp.logical_and(ok, term)
        return ok

    peers = [("chan", i_chan, n_chan, k) for k in range(1, n_chan)]
    peers += [("col", i_col, n_col, k) for k in range(1, n_col)]
    peers += [("row", i_row, n_row, k) for k in range(1, n_row)]

    barrier = pltpu.get_barrier_semaphore()

    def greets(d):
        if d in (LEFT, RIGHT):
            return None
        ok = exists(*DIRS[d])
        if d == UP:
            ok = jnp.logical_and(ok, i_chan == 0)
        if d == DOWN:
            ok = jnp.logical_and(ok, i_chan == n_chan - 1)
        return ok

    for d in range(8):
        if greets(d) is not None:

            @pl.when(greets(d))
            def _():
                pl.semaphore_signal(barrier, inc=1, device_id=place(*DIRS[d]), device_id_type=pl.DeviceIdType.MESH)

    for axis, at, count, k in peers:
        pl.semaphore_signal(
            barrier, inc=1, device_id={axis: (at + k) % count}, device_id_type=pl.DeviceIdType.MESH
        )

    def barrier_wait():
        total = jnp.int32(len(peers))
        for d in range(8):
            if greets(d) is not None:
                total = total + greets(d).astype(jnp.int32)
        pl.semaphore_wait(barrier, total)

    def copy(stage, d, src, dst):
        return pltpu.make_async_remote_copy(
            src_ref=src,
            dst_ref=dst,
            send_sem=send_sem.at[stage, d],
            recv_sem=recv_sem.at[stage, d],
            device_id=place(*DIRS[d]),
            device_id_type=pl.DeviceIdType.MESH,
        )

    def start(stage, plan):
        for d, (src, dst) in enumerate(plan):

            @pl.when(exists(*DIRS[d]))
            def _():
                copy(stage, d, src, dst).start()

    def arrive(stage, plan):
        for d, (src, dst) in enumerate(plan):
            back = DIRS[OPP[d]]

            @pl.when(exists(*back))
            def _():
                copy(stage, d, src, dst).wait_recv()

            @pl.when(jnp.logical_not(exists(*back)))
            def _():
                dst[...] = jnp.zeros(dst.shape, dst.dtype)

    def drain(stage, plan):
        for d, (src, dst) in enumerate(plan):

            @pl.when(exists(*DIRS[d]))
            def _():
                copy(stage, d, src, dst).wait_send()

    plan0 = [
        (su0, rd0), (sd0, ru0), (se0, rr0), (se0, rl0),
        (seu, rc0.at[3]), (seu, rc0.at[2]), (sed, rc0.at[1]), (sed, rc0.at[0]),
    ]

    def side_plan(up, down, side, hs):
        return [
            up, down, (side, hs.at[1]), (side, hs.at[0]),
            (side, hs.at[5]), (side, hs.at[4]), (side, hs.at[3]), (side, hs.at[2]),
        ]

    plan1 = [
        side_plan(
            (pool1.at[f, pl.ds(2, 2)], pool1.at[f, pl.ds(10, 2)]),
            (pool1.at[f, pl.ds(8, 2)], pool1.at[f, pl.ds(0, 2)]),
            se1.at[f], hs1.at[f],
        )
        for f in range(2)
    ]
    plan2 = [
        side_plan((pool2.at[f, 0], rd2.at[f]), (pool2.at[f, 1], ru2.at[f]), se2.at[f], hs2.at[f])
        for f in range(2)
    ]
    plan3 = side_plan((d3.at[0], rd3), (d3.at[1], ru3), se3, hs3)
    plan4 = side_plan((d2.at[pl.ds(2, 2)], d2.at[pl.ds(10, 2)]), (d2.at[pl.ds(8, 2)], d2.at[pl.ds(0, 2)]), se4, hs4)
    plan5 = side_plan((d1.at[0], rd5), (d1.at[15], ru5), se5, hs5)

    for f, img in enumerate((img0, img1)):
        for c in range(3):
            v = ((img[c] - OFFSETS[c]) * (1.0 / SPREADS[c])).astype(BF)
            pf[3 * f + c, 8:72, :] = v.astype(F32)
            edge = jnp.where(
                lanes((64, 128)) < 4, v[:, :128].astype(F32), roll(v[:, 896:].astype(F32), 8)
            )
            se0[f * 192 + 64 * c : f * 192 + 64 * c + 64, :] = edge.astype(BF)
    for buf, edge, at in ((su0, seu, 8), (sd0, sed, 68)):
        tmp[...] = jnp.zeros(tmp.shape, F32)
        for f in range(2):
            for c in range(3):
                tmp[16 * f + 4 * c : 16 * f + 4 * c + 4, :] = pf[3 * f + c, at : at + 4, :]
        v = tmp[...]
        buf[...] = v.astype(BF)
        edge[...] = jnp.where(lanes((32, 128)) < 4, v[:, :128], roll(v[:, 896:], 8)).astype(BF)

    barrier_wait()
    start(0, plan0)

    def shard_copy(k):
        rows = pl.ds(i_chan * 96, 96)
        return pltpu.make_async_remote_copy(
            src_ref=w3s,
            dst_ref=w3t.at[rows],
            send_sem=wsend.at[k - 1],
            recv_sem=wrecv.at[k - 1],
            device_id={"chan": (i_chan + k) % n_chan},
            device_id_type=pl.DeviceIdType.MESH,
        )

    for k in range(1, n_chan):
        shard_copy(k).start()
    w3t[pl.ds(pl.multiple_of(i_chan * 96, 32), 96), :] = w3s[...]

    for src, dst in ((b1, cb1), (b2, cb2), (b3, cb3), (l1, cl1), (l2, cl2), (l3, cl3)):
        dst[...] = jnp.transpose(jnp.broadcast_to(src[...], (128, src.shape[1])))
    la[...] = jnp.zeros(la.shape, F32)

    for px in range(8):
        at = lax.broadcasted_iota(jnp.int32, (1024, 128), 0)
        lane = lanes((1024, 128))
        want = 8 * (2 * (lane % 64) + lane // 64) + px
        sel[:, 128 * px : 128 * px + 128] = jnp.where(at == want, 1.0, 0.0).astype(BF)

    arrive(0, plan0)
    for buf, at in ((ru0, 4), (rd0, 72)):
        tmp[...] = buf[...].astype(F32)
        for f in range(2):
            for c in range(3):
                pf[3 * f + c, at : at + 4, :] = tmp[16 * f + 4 * c : 16 * f + 4 * c + 4, :]
    for s, (mid, up, down) in enumerate(((rl0, 0, 2), (rr0, 1, 3))):
        for f in range(2):
            for c in range(3):
                ef[s, 3 * f + c, 8:72, :] = mid[f * 192 + 64 * c : f * 192 + 64 * c + 64, :].astype(F32)
        for corner, at in ((up, 4), (down, 72)):
            tmp[:, :128] = rc0[corner].astype(F32)
            for f in range(2):
                for c in range(3):
                    ef[s, 3 * f + c, at : at + 4, :] = tmp[16 * f + 4 * c : 16 * f + 4 * c + 4, :128]

    def pixels(f):
        for r in range(8):
            for c in range(3):
                rows = slice((r * 3 + c) * 16, (r * 3 + c) * 16 + 16)
                lw[rows, :] = pf[3 * f + c, 8 * r + 4 : 8 * r + 20, :].astype(BF)
                for s in range(2):
                    ew[s, rows, :] = ef[s, 3 * f + c, 8 * r + 4 : 8 * r + 20, :]
        for pp in range(4):
            both = dot(lw[...], sel[:, 256 * pp : 256 * pp + 256])
            for px in (2 * pp, 2 * pp + 1):
                x = both[:, 128 * (px % 2) : 128 * (px % 2) + 128]
                if px >= 4:
                    other = shifted(x, -1)
                    other = jnp.where(lanes(x.shape) == 0, roll(ew[0], -px), other)
                    wx = px - 4
                else:
                    other = shifted(x, 1)
                    other = jnp.where(lanes(x.shape) == 127, roll(ew[1], 127 - px), other)
                    wx = 12 + px
                for w, v in ((4 + px, x), (wx, other)):
                    v = v.astype(BF)
                    for r in range(8):
                        x1[r % 4, 48 * w : 48 * w + 48, 128 * (r // 4) : 128 * (r // 4) + 128] = v[48 * r : 48 * r + 48]

    def silu(v):
        sigma = 0.5 * jnp.tanh(0.5 * v) + 0.5
        return v * sigma, sigma

    def layer_one(f):
        def body(i, _):
            out = dot(wb1[...], x1[i])
            for h in range(2):
                acc = None
                for ph in range(4):
                    v = out[64 * ph : 64 * ph + 64, 128 * h : 128 * h + 128] + cb1[...]
                    feat, sigma = silu(v)
                    n = (i + 4 * h) * 4 + ph
                    f1[f, n] = feat
                    if f == 0:
                        sl1[n] = sigma * (1.0 + v * (1.0 - sigma))
                    acc = feat if acc is None else acc + feat
                pool1[f, 2 + i + 4 * h] = (0.25 * acc).astype(BF)
            return 0

        lax.fori_loop(0, 4, body, 0)

    def pack_columns(rows, side):
        channels = side.shape[0]
        for at in range(0, channels, 64):
            acc = jnp.zeros((64, 128), F32)
            lane = lanes((64, 128)) % 64
            for r in range(8):
                x = rows(r, at).astype(F32)
                acc = jnp.where(lane == r + 2, roll(x, r + 2), acc)
                acc = jnp.where(lane == 16 + r + 2, roll(x, 16 + r + 2 - 63), acc)
            side[at : at + 64, :] = acc.astype(BF)

    def merged(hs, at, size, step, top, bottom, base):
        lane = lanes((size, 128)) % 64
        sides = []
        for s, first in ((1, 0), (0, base)):
            mid = hs[s, at : at + size, :].astype(F32)
            up = roll(hs[2 + s, at : at + size, :].astype(F32), -step)
            down = roll(hs[4 + s, at : at + size, :].astype(F32), step)
            v = jnp.where(lane < first + top, up, jnp.where(lane < first + bottom, mid, down))
            sides.append(v)
        return jnp.where(lane < base, sides[0], sides[1])

    def layer_two_operand(f):
        lane = lanes((64, 128))
        halo = merged(hs1.at[f], 0, 64, 8, 2, 10, 16)
        for rr in range(12):
            x = pool1[f, rr].astype(F32)
            right = roll(halo, 63 - rr)
            left = roll(halo, -16 - rr)
            cols = (
                jnp.where(lane % 64 == 0, left, shifted(x, -2)),
                jnp.where(lane == 0, roll(left, 64), shifted(x, -1)),
                x,
                jnp.where(lane == 127, roll(right, 64), shifted(x, 1)),
                jnp.where(lane % 64 == 63, right, shifted(x, 2)),
            )
            for e, v in enumerate(cols):
                v = v.astype(BF)
                if rr < 8:
                    x2[320 * rr + 64 * e : 320 * rr + 64 * e + 64, :128] = v
                if rr >= 4:
                    x2[320 * (rr - 4) + 64 * e : 320 * (rr - 4) + 64 * e + 64, 128:] = v

    def layer_two(f):
        low = lanes((64, 128)) < 64
        for i in range(4):
            out = dot(w2t[...], x2[320 * i : 320 * i + 1600, :])
            for h in range(2):
                for k in range(3):
                    rows = slice(64 * k, 64 * k + 64)
                    v = out[rows, 128 * h : 128 * h + 128] + cb2[rows]
                    feat, sigma = silu(v)
                    f2[f, i + 4 * h, rows] = feat
                    if f == 0:
                        sl2[i + 4 * h, rows] = sigma * (1.0 + v * (1.0 - sigma))
                    if i % 2 == 1:
                        both = f2[f, i - 1 + 4 * h, rows] + feat
                        mean = 0.25 * (both + roll(both, 64))
                        if i == 1:
                            keep[h, rows] = mean
                        else:
                            pool2[f, h, rows] = jnp.where(low, keep[h, rows], mean).astype(BF)

    def pack_ends(tiles, side):
        channels = side.shape[0]
        for at in range(0, channels, 64):
            lane = lanes((64, 128))
            acc = jnp.zeros((64, 128), F32)
            for r in range(4):
                x = tiles[r // 2, at : at + 64, :].astype(F32)
                first = 64 * (r % 2)
                for src, dst in ((0, r + 1), (0, 64 + r), (63, 16 + r + 1), (63, 80 + r)):
                    acc = jnp.where(lane == dst, roll(x, dst - src - first), acc)
            side[at : at + 64, :] = acc.astype(BF)

    def merged_ends(hs, at):
        lane = lanes((64, 128))
        sides = []
        for s, first in ((1, 0), (0, 16)):
            mid = hs[s, at : at + 64, :].astype(F32)
            up = roll(hs[2 + s, at : at + 64, :].astype(F32), -4)
            down = roll(hs[4 + s, at : at + 64, :].astype(F32), 4)
            v = jnp.where(lane == first, up, jnp.where(lane == first + 5, down, mid))
            sides.append(jnp.where(lane == 64 + first + 4, down, v))
        return jnp.where(lane % 64 < 16, sides[0], sides[1])

    def layer_three_operand(tiles, from_up, from_down, hs, dst):
        channels = tiles.shape[1]
        for at in range(0, channels, 64):
            rows = slice(at, at + 64)
            lane = lanes((64, 128))
            low = lane < 64
            halo = merged_ends(hs, at)
            b = tiles[0, rows].astype(F32)
            d = tiles[1, rows].astype(F32)
            b_swap, d_swap = roll(b, 64), roll(d, 64)
            a = jnp.where(low, roll(from_up[rows].astype(F32), 64), b_swap)
            c = jnp.where(low, b_swap, d_swap)
            e = jnp.where(low, d_swap, roll(from_down[rows].astype(F32), 64))
            for rr, (x, spots) in enumerate(
                ((a, ((0, 0),)), (b, ((1, 0),)), (c, ((0, 1), (2, 0))), (d, ((1, 1),)), (e, ((2, 1),)))
            ):
                left = jnp.where(lane % 64 == 0, roll(halo, -16 - rr), roll(x, 1))
                right = jnp.where(lane % 64 == 63, roll(halo, 63 - rr), roll(x, 127))
                for dx, v in enumerate((left, x, right)):
                    v = v.astype(BF)
                    for dy, half in spots:
                        base = (dy * 3 + dx) * channels + at
                        dst[base : base + 64, 128 * half : 128 * half + 128] = v

    def layer_three(f):
        out = dot(w3t[...], x3[f])
        for h in range(2):
            for k in range(6):
                rows = slice(64 * k, 64 * k + 64)
                v = out[rows, 128 * h : 128 * h + 128] + cb3[rows]
                feat, sigma = silu(v)
                f3[f, h, rows] = feat
                if f == 0:
                    sl3[h, rows] = sigma * (1.0 + v * (1.0 - sigma))

    def local_terms(feats, n, weights, factor, count, finish):
        chunks = weights.shape[0] // 64
        rows = [slice(64 * k, 64 * k + 64) for k in range(chunks)]
        sums = [jnp.zeros((1, 128), F32)] * 2
        for f in range(2):
            for k in range(chunks):
                v = feats[f, n, rows[k]]
                sums[f] = sums[f] + jnp.sum(v * v, axis=0, keepdims=True)
        first, second = lax.rsqrt(sums[0] + EPSILON), lax.rsqrt(sums[1] + EPSILON)
        inner = jnp.zeros((1, 128), F32)
        total = jnp.zeros((1, 128), F32)
        for k in range(chunks):
            v = feats[0, n, rows[k]]
            differ = v * first - feats[1, n, rows[k]] * second
            slope = weights[rows[k]] * differ
            total = total + jnp.sum(slope * differ, axis=0, keepdims=True)
            inner = inner + jnp.sum(v * slope, axis=0, keepdims=True)
        la[0:1, :] = la[0:1, :] + total * (1.0 / count)
        scale = 2.0 * factor * first
        cubed = 2.0 * factor * first * first * first * inner
        for k in range(chunks):
            v = feats[0, n, rows[k]]
            slope = weights[rows[k]] * (v * first - feats[1, n, rows[k]] * second)
            finish(k, rows[k], scale * slope - v * cubed)

    for f in range(2):
        pixels(f)
        layer_one(f)
        pack_columns(lambda r, at: pool1[f, 2 + r], se1.at[f])
        start(1 + f, plan1[f])
    for f in range(2):
        arrive(1 + f, plan1[f])
        layer_two_operand(f)
        layer_two(f)
        pack_ends(pool2.at[f], se2.at[f])
        start(3 + f, plan2[f])
    for k in range(1, n_chan):
        shard_copy(k).wait_recv()
    for f in range(2):
        arrive(3 + f, plan2[f])
        layer_three_operand(pool2.at[f], ru2.at[f], rd2.at[f], hs2.at[f], x3.at[f])
        layer_three(f)

    pixel_count = 64 * n_tile * 1024 * n_col

    for h in range(2):

        def finish_three(k, rows, dfeat):
            d3[h, rows] = (dfeat * sl3[h, rows]).astype(BF)

        local_terms(f3, h, cl3, 256.0, pixel_count // 256, finish_three)
    pack_ends(d3, se3)
    start(5, plan3)

    def terms_two(n, _):
        def finish_two(k, rows, dfeat):
            f2[0, n, rows] = dfeat

        local_terms(f2, n, cl2, 64.0, pixel_count // 64, finish_two)
        return 0

    lax.fori_loop(0, 8, terms_two, 0)

    def terms_one(n, _):
        def finish_one(k, rows, dfeat):
            f1[0, n, rows] = dfeat

        local_terms(f1, n, cl1, 16.0, pixel_count // 16, finish_one)
        return 0

    lax.fori_loop(0, 32, terms_one, 0)

    def loss_copy(axis, k):
        which = ("col", "chan", "row").index(axis)
        slots = (lsa, lsb, lsc)[which]
        at, count = ((i_col, n_col), (i_chan, n_chan), (i_row, n_row))[which]
        return pltpu.make_async_remote_copy(
            src_ref=la,
            dst_ref=slots.at[k - 1],
            send_sem=lsend.at[which, k - 1],
            recv_sem=lrecv.at[which, k - 1],
            device_id={axis: (at + k) % count},
            device_id_type=pl.DeviceIdType.MESH,
        )

    def loss_start(axis, count):
        for k in range(1, count):
            loss_copy(axis, k).start()

    def loss_finish(axis, count, slots):
        for k in range(1, count):
            loss_copy(axis, k).wait()
        total = la[...]
        for k in range(1, count):
            total = total + slots[k - 1]
        la[...] = total

    loss_start("col", n_col)
    eye = jnp.where(
        lax.broadcasted_iota(jnp.int32, (128, 128), 0) == lanes((128, 128)), 1.0, 0.0
    ).astype(BF)
    for at in range(0, 1728, 128):
        size = min(128, 1728 - at)
        part = lax.dot_general(
            eye[:size, :size], w3t[:, at : at + size], (((1,), (1,)), ((), ())), preferred_element_type=F32
        )
        w3n[at : at + size, :] = part.astype(BF)

    arrive(5, plan3)
    layer_three_operand(d3, ru3, rd3, hs3, x3d)
    acc = None
    for tap in range(9):
        part = dot(w3n[192 * (8 - tap) : 192 * (8 - tap) + 192, :], x3d[384 * tap : 384 * tap + 384, :])
        acc = part if acc is None else acc + part
    dp2[...] = acc
    loss_finish("col", n_col, lsa)
    loss_start("chan", n_chan)

    for r in range(8):
        for k in range(3):
            rows = slice(64 * k, 64 * k + 64)
            t = dp2[rows, 128 * (r // 4) : 128 * (r // 4) + 128]
            low = lanes((64, 128)) < 64
            swap = roll(t, 64)
            wide = jnp.where(low, t, swap) if (r // 2) % 2 == 0 else jnp.where(low, swap, t)
            d2[2 + r, rows] = ((f2[0, r, rows] + 0.25 * wide) * sl2[r, rows]).astype(BF)
    pack_columns(lambda r, at: d2[2 + r, at : at + 64], se4)
    start(6, plan4)
    arrive(6, plan4)
    for rr in range(12):
        v = d2[rr]
        if rr < 8:
            x4[192 * rr : 192 * rr + 192, :128] = v
        if rr >= 4:
            x4[192 * (rr - 4) : 192 * (rr - 4) + 192, 128:] = v
    for at in range(0, 192, 64):
        halo = merged(hs4, at, 64, 8, 2, 10, 16)
        for dy in range(5):
            xh[192 * dy + at : 192 * dy + at + 64, :] = roll(halo, -dy).astype(BF)
    acc = None
    for dy in range(5):
        part = dot(w2n[320 * (4 - dy) : 320 * (4 - dy) + 320, :], xh[192 * dy : 192 * dy + 192, :])
        acc = part if acc is None else acc + part
    yh[...] = acc
    loss_finish("chan", n_chan, lsb)
    loss_start("row", n_row)
    lane = lanes((64, 128))
    for i in range(4):
        acc = None
        for dy in range(5):
            part = dot(
                w2n[320 * (4 - dy) : 320 * (4 - dy) + 320, :],
                x4[192 * (i + dy) : 192 * (i + dy) + 192, :],
            )
            acc = part if acc is None else acc + part
        yb[...] = acc
        for h in range(2):
            r = i + 4 * h

            def piece(e, src=None):
                if src is None:
                    return yb[64 * (2 - e) : 64 * (2 - e) + 64, 128 * h : 128 * h + 128]
                return yh[64 * (2 - e) : 64 * (2 - e) + 64, :]

            total = piece(0)
            total = total + jnp.where(lane == 127, roll(piece(1, 1), 127 - r), shifted(piece(1), 1))
            total = total + jnp.where(lane % 64 == 63, roll(piece(2, 1), 63 - r), shifted(piece(2), 2))
            total = total + jnp.where(lane == 0, roll(piece(-1, 1), -80 - r), shifted(piece(-1), -1))
            total = total + jnp.where(lane % 64 == 0, roll(piece(-2, 1), -16 - r), shifted(piece(-2), -2))
            total = 0.25 * total
            for py in range(2):
                for px in range(2):
                    n = 4 * r + 2 * py + px
                    d1[2 * r + py, 64 * px : 64 * px + 64] = ((f1[0, n] + total) * sl1[n]).astype(BF)

    acc = jnp.zeros((64, 128), F32)
    for cr in range(16):
        acc = jnp.where(lane == cr + 1, roll(d1[cr, :64].astype(F32), cr + 1), acc)
        acc = jnp.where(lane == cr + 33, roll(d1[cr, 64:].astype(F32), cr + 33 - 127), acc)
    se5[...] = acc.astype(BF)
    start(7, plan5)
    arrive(7, plan5)
    sides = []
    for s, first in ((1, 0), (0, 32)):
        mid = hs5[s].astype(F32)
        up = roll(hs5[2 + s].astype(F32), -16)
        down = roll(hs5[4 + s].astype(F32), 16)
        sides.append(jnp.where(lane == first, up, jnp.where(lane == first + 17, down, mid)))
    halo = jnp.where(lane < 32, sides[0], sides[1])
    for n in range(18):
        src = ru5 if n == 0 else rd5 if n == 17 else d1.at[n - 1]
        zero, one = src[:64], src[64:]
        before = jnp.where(lane == 0, roll(halo, -32 - n), shifted(one.astype(F32), -1)).astype(BF)
        after = jnp.where(lane == 127, roll(halo, 127 - n), shifted(zero.astype(F32), 1)).astype(BF)
        for g, v in enumerate((before, zero, one, after)):
            if n < 10:
                x5[256 * n + 64 * g : 256 * n + 64 * g + 64, :128] = v
            if n >= 8:
                x5[256 * (n - 8) + 64 * g : 256 * (n - 8) + 64 * g + 64, 128:] = v
    for i in range(4):
        out = dot(wb1b[...], x5[512 * i : 512 * i + 1024, :])
        for h in range(2):
            r = i + 4 * h
            for px in range(8):
                for c in range(3):
                    at = px * 24 + c * 8
                    bf[64 * c + 8 * r : 64 * c + 8 * r + 8, 128 * px : 128 * px + 128] = out[
                        at : at + 8, 128 * h : 128 * h + 128
                    ]
    loss_finish("row", n_row, lsc)
    loss[...] = jnp.sum(la[0:1, :], axis=1, keepdims=True)
    planes = bf[...].astype(BF)
    for part in range(4):
        cols = slice(256 * part, 256 * part + 256)
        out = lax.dot_general(planes, sel[cols, :], (((1,), (1,)), ((), ())), preferred_element_type=F32)
        for c in range(3):
            grad[c, :, cols] = out[64 * c : 64 * c + 64] * (1.0 / SPREADS[c])

    drain(0, plan0)
    for f in range(2):
        drain(1 + f, plan1[f])
        drain(3 + f, plan2[f])
    drain(5, plan3)
    drain(6, plan4)
    drain(7, plan5)
    for k in range(1, n_chan):
        shard_copy(k).wait_send()


def block_kernel(kernel_one, flip):
    base = kernel_one.reshape(3, 3, 3, 4, 4, 64)
    if flip:
        base = base[::-1, ::-1]
    rows = []
    for cy in range(2):
        rows.append(
            jnp.stack(
                [jnp.pad(base, ((cy, 1 - cy), (cx, 1 - cx)) + ((0, 0),) * 4) for cx in range(2)]
            )
        )
    return jnp.stack(rows)


def local(
    image_gen, image_ref, kernel_one, bias_one, kernel_two, bias_two, kernel_three, bias_three,
    lin_first, lin_second, lin_third,
):
    n_row, n_col, n_chan = lax.axis_size("row"), lax.axis_size("col"), lax.axis_size("chan")
    wb1 = block_kernel(kernel_one, False).transpose(0, 1, 7, 3, 6, 4, 2, 5).reshape(256, 768)
    wb1b = block_kernel(kernel_one, True).transpose(1, 6, 4, 0, 5, 2, 3, 7).reshape(192, 1024)
    w2n = kernel_two.reshape(1600, 192)
    w3s = kernel_three.reshape(1728, 96).T
    rows = [v.reshape(1, -1) for v in (bias_one, bias_two, bias_three, lin_first, lin_second, lin_third)]
    V = pltpu.VMEM
    scratch = dict(
        sel=V((1024, 1024), BF), pf=V((6, 80, 1024), F32), ef=V((2, 6, 80, 128), F32),
        tmp=V((32, 1024), F32), lw=V((384, 1024), BF), ew=V((2, 384, 128), F32),
        x1=V((4, 768, 256), BF), f1=V((2, 32, 64, 128), F32), sl1=V((32, 64, 128), F32),
        pool1=V((2, 12, 64, 128), BF), x2=V((2560, 256), BF), f2=V((2, 8, 192, 128), F32),
        sl2=V((8, 192, 128), F32), keep=V((2, 192, 128), F32), pool2=V((2, 2, 192, 128), BF),
        x3=V((2, 1728, 256), BF), f3=V((2, 2, 384, 128), F32), sl3=V((2, 384, 128), F32),
        d3=V((2, 384, 128), BF), x3d=V((3456, 256), BF), w3t=V((384, 1728), BF), w3n=V((1728, 384), BF),
        dp2=V((192, 256), F32), d2=V((12, 192, 128), BF), x4=V((1536, 256), BF), yb=V((320, 256), F32),
        xh=V((960, 128), BF), yh=V((320, 128), F32), d1=V((16, 128, 128), BF), x5=V((2560, 256), BF),
        bf=V((192, 1024), F32), cb1=V((64, 128), F32), cb2=V((192, 128), F32), cb3=V((384, 128), F32),
        cl1=V((64, 128), F32), cl2=V((192, 128), F32), cl3=V((384, 128), F32), la=V((8, 128), F32),
        lsa=V((max(n_col - 1, 1), 8, 128), F32), lsb=V((max(n_chan - 1, 1), 8, 128), F32),
        lsc=V((max(n_row - 1, 1), 8, 128), F32),
        su0=V((32, 1024), BF), sd0=V((32, 1024), BF), se0=V((384, 128), BF), seu=V((32, 128), BF),
        sed=V((32, 128), BF), ru0=V((32, 1024), BF), rd0=V((32, 1024), BF), rl0=V((384, 128), BF),
        rr0=V((384, 128), BF), rc0=V((4, 32, 128), BF),
        se1=V((2, 64, 128), BF), hs1=V((2, 6, 64, 128), BF), se2=V((2, 192, 128), BF),
        hs2=V((2, 6, 192, 128), BF), ru2=V((2, 192, 128), BF), rd2=V((2, 192, 128), BF),
        se3=V((384, 128), BF), hs3=V((6, 384, 128), BF), ru3=V((384, 128), BF), rd3=V((384, 128), BF),
        se4=V((192, 128), BF), hs4=V((6, 192, 128), BF), se5=V((64, 128), BF), hs5=V((6, 64, 128), BF),
        ru5=V((128, 128), BF), rd5=V((128, 128), BF),
        send_sem=pltpu.SemaphoreType.DMA((STAGES, 8)), recv_sem=pltpu.SemaphoreType.DMA((STAGES, 8)),
        wsend=pltpu.SemaphoreType.DMA((n_chan,)), wrecv=pltpu.SemaphoreType.DMA((n_chan,)),
        lsend=pltpu.SemaphoreType.DMA((3, 8)), lrecv=pltpu.SemaphoreType.DMA((3, 8)),
    )
    vmem = pl.BlockSpec(memory_space=pltpu.VMEM)
    grad, loss = pl.pallas_call(
        kernel,
        out_shape=(
            jax.ShapeDtypeStruct(image_gen.shape, F32),
            jax.ShapeDtypeStruct((1, 1), F32),
        ),
        in_specs=[vmem] * 13,
        out_specs=(vmem, vmem),
        scratch_shapes=list(scratch.values()),
        compiler_params=pltpu.CompilerParams(
            collective_id=0, has_side_effects=True, vmem_limit_bytes=62 * 1024 * 1024
        ),
        name="whole",
    )(image_gen, image_ref, wb1, w2n.T, w2n, w3s, wb1b, *rows)
    return (grad, loss.reshape(()))


def solution(mesh):
    rows = ("row", "chan")
    in_specs = (
        P(None, rows, "col"), P(None, rows, "col"), P(), P(), P(), P(),
        P(None, None, None, "chan"), P(), P(), P(), P(),
    )
    out_specs = (P(None, rows, "col"), P())
    return jax.shard_map(local, mesh=mesh, in_specs=in_specs, out_specs=out_specs, check_vma=False)
```

profile of v0, /device:TPU:25, one launch (start us, length us, event | category | flops | bytes accessed | tf_op | source)
XLA Modules:
  0.0 91.2 jit_solution(646586628574890186)
XLA Ops:
  0.6 0.9 %rev.3 = bf16[3,3,3,4,4,64]{5,4,3,2,1,0:T(4,128)(2,1)S(1)} reverse(bf16[3,3,3,4,4,64]{5,4,3,2,1,0:T(4,128)(2,1)} %bitcast.45), dimensions={0,1} | reverse | bytes 110592 | tf_op jit(solution)/shard_map/rev | solution.py:631
  1.6 0.2 pad_bitcast_fusion.3
  1.8 0.7 maximum_bitcast_fusion.4
  2.5 0.7 maximum_bitcast_fusion.1
  3.2 0.4 copy.32
  3.6 0.0 copy-start.2
  3.6 1.3 %reshape.45.wb1b = bf16[192,1024]{1,0:T(8,128)(2,1)} reshape(bf16[2,4,3,2,4,4,4,64]{7,6,5,4,3,2,1,0:T(4,128)(2,1)S(1)} %copy.32) | data formatting | bytes 786432 | tf_op jit(solution)/shard_map/reshape | solution.py:648
  4.9 0.0 copy-done.2
  4.9 0.2 pad_bitcast_fusion.7
  5.2 0.7 maximum_bitcast_fusion.2
  5.9 0.7 maximum_bitcast_fusion
  6.5 0.8 copy.30
  7.3 0.0 copy-start
  7.4 0.5 reshape.42
  7.8 0.9 %copy.33.wb1 = bf16[256,768]{1,0:T(8,128)(2,1)} copy(bf16[256,768]{0,1:T(8,128)(2,1)S(1)} %reshape.42) | data formatting | bytes 786432 | tf_op jit(solution)/shard_map/reshape | solution.py:647
  8.8 0.0 copy-done
  8.8 1.1 %copy.34.w2t = bf16[192,1600]{1,0:T(8,128)(2,1)} copy(bf16[192,1600]{0,1:T(8,128)(2,1)S(1)} %bitcast.42) | data formatting | bytes 1228800 | tf_op jit(solution)/shard_map/transpose | solution.py:693
  9.9 0.0 copy-done.1
  9.9 1.0 %copy.31 = bf16[1728,96]{0,1:T(8,128)(2,1)} copy(bf16[1728,96]{1,0:T(8,128)(2,1)S(1)} %bitcast.44) | data formatting | bytes 663552 | tf_op jit(solution)/shard_map/reshape | solution.py:650
  10.9 0.6 reshape.48.b3
  11.5 0.1 copy-done.4
  11.6 0.6 reshape.51.l3
  12.1 75.2 %whole.1 = (f32[3,64,1024]{2,1,0:T(8,128)}, f32[1,1]{1,0:T(1,128)}) custom-call(f32[3,64,1024]{2,1,0:T(8,128)} %img0.1, f32[3,64,1024]{2,1,0:T(8,128)} %img1.1, bf16[256,768]{1,0:T(8,128)(2,1)} %copy.33.wb1, bf16[192,1600]{1,0:T(8,128)(2,1)} %copy.34.w2t, bf16[1600,192]{1,0:T(8,128)(2,1)} %bitcast.41, bf16[96,1728]{1,0:T(8,128)(2,1)} %bitcast.43, ...), custom_call_target="tpu_custom_call" | custom-call | tf_op jit(solution)/shard_map/whole/pallas_call | solution.py:680
  87.3 2.1 %copy.37 = f32[3,64,1024]{2,1,0:T(8,128)} copy(f32[3,64,1024]{2,1,0:T(8,128)} %get-tuple-element.20) | data formatting | bytes 1572864
  (4 shorter events, 0.0 us)
Async XLA Ops:
  3.6 1.3 %copy-start.2 = (bf16[3,3,48,64]{3,2,1,0:T(8,128)(2,1)S(1)}, bf16[3,3,48,64]{3,2,1,0:T(8,128)(2,1)}, u32[]{:S(2)}) copy-start(bf16[3,3,48,64]{3,2,1,0:T(8,128)(2,1)} %param.13) | copy-start | bytes 165892
  7.3 1.4 %copy-start = (bf16[5,5,64,192]{3,2,1,0:T(8,128)(2,1)S(1)}, bf16[5,5,64,192]{3,2,1,0:T(8,128)(2,1)}, u32[]{:S(2)}) copy-start(bf16[5,5,64,192]{3,2,1,0:T(8,128)(2,1)} %param.15) | copy-start | bytes 1843204
  8.8 1.1 %copy-start.1 = (bf16[3,3,192,96]{3,2,1,0:T(8,128)(2,1)S(1)}, bf16[3,3,192,96]{3,2,1,0:T(8,128)(2,1)}, u32[]{:S(2)}) copy-start(bf16[3,3,192,96]{3,2,1,0:T(8,128)(2,1)} %param.17) | copy-start | bytes 995332
  9.9 1.0 %copy-start.3 = (f32[384]{0:T(512)S(1)}, f32[384]{0:T(512)}, u32[]{:S(2)}) copy-start(f32[384]{0:T(512)} %param.18) | copy-start | bytes 4612
  10.9 0.7 copy-start.4
where the time goes:
time: 92.6 us; the launch traced here: 91.2 us
  Pallas kernels  75.2 us (81%)
  local copies, waits for them, and re-layouts  10.8 us (12%)
  other arithmetic  2.68 us (3%)
  between operations  2.47 us (3%)
    pallas_call x1, Pallas kernels, local(): pl.pallas_call(kernel, out_shape=(jax.ShapeDtypeStruct(image_gen.shape, F...  75.2 us
    unnamed x11, local copies, waits for them, and re-layouts  2.2 us

commit v1 on v0

--- a/solution.py
+++ b/solution.py
@@ -40,14 +40,15 @@
 
 
 def kernel(
-    img0, img1, wb1, w2t, w2n, w3s, wb1b, b1, b2, b3, l1, l2, l3,
+    img0_hbm, img1_hbm, k1_hbm, k2_hbm, k3_hbm, b1, b2, b3, l1, l2, l3,
     grad, loss,
+    img, k1, w2n, k3, kpair, sela, wb1, wb1b, w2t,
     sel, pf, ef, tmp, lw, ew, x1, f1, sl1, pool1, x2, f2, sl2, keep, pool2, x3,
-    f3, sl3, d3, x3d, w3t, w3n, dp2, d2, x4, yb, xh, yh, d1, x5, bf,
+    f3, sl3, d3, x3d, w3t, w3n, dp2, d2, x4, yb, xh, yh, d1, x5, bf, hb,
     cb1, cb2, cb3, cl1, cl2, cl3, la, lsa, lsb, lsc,
     su0, sd0, se0, seu, sed, ru0, rd0, rl0, rr0, rc0,
-    se1, hs1, se2, hs2, ru2, rd2, se3, hs3, ru3, rd3, se4, hs4, se5, hs5, ru5, rd5,
-    send_sem, recv_sem, wsend, wrecv, lsend, lrecv,
+    se1, hs1, se2, hs2, su2, sd2, ru2, rd2, se3, hs3, su3, sd3, ru3, rd3, se4, hs4, se5, hs5, ru5, rd5,
+    send_sem, recv_sem, wsend, wrecv, lsend, lrecv, in_sem,
 ):
     n_row, n_col, n_chan = lax.axis_size("row"), lax.axis_size("col"), lax.axis_size("chan")
     i_row, i_col, i_chan = lax.axis_index("row"), lax.axis_index("col"), lax.axis_index("chan")
@@ -73,6 +74,8 @@
     peers = [("chan", i_chan, n_chan, k) for k in range(1, n_chan)]
     peers += [("col", i_col, n_col, k) for k in range(1, n_col)]
     peers += [("row", i_row, n_row, k) for k in range(1, n_row)]
+    far = {"row": i_row + 1 - 2 * (i_row % 2), "chan": (i_chan + 2) % n_chan}
+    near = {"chan": i_chan + 1 - 2 * (i_chan % 2)}
 
     barrier = pltpu.get_barrier_semaphore()
 
@@ -93,13 +96,27 @@
             def _():
                 pl.semaphore_signal(barrier, inc=1, device_id=place(*DIRS[d]), device_id_type=pl.DeviceIdType.MESH)
 
+    loads = [
+        pltpu.make_async_copy(src, dst, in_sem.at[n])
+        for n, (src, dst) in enumerate(
+            (
+                (img0_hbm, img.at[0]), (img1_hbm, img.at[1]), (k3_hbm, k3), (k1_hbm, k1), (k2_hbm, w2n),
+            )
+        )
+    ]
+    for load in loads:
+        load.start()
+
     for axis, at, count, k in peers:
         pl.semaphore_signal(
             barrier, inc=1, device_id={axis: (at + k) % count}, device_id_type=pl.DeviceIdType.MESH
         )
 
+    if n_chan > 1:
+        pl.semaphore_signal(barrier, inc=1, device_id=far, device_id_type=pl.DeviceIdType.MESH)
+
     def barrier_wait():
-        total = jnp.int32(len(peers))
+        total = jnp.int32(len(peers) + (1 if n_chan > 1 else 0))
         for d in range(8):
             if greets(d) is not None:
                 total = total + greets(d).astype(jnp.int32)
@@ -161,21 +178,28 @@
         for f in range(2)
     ]
     plan2 = [
-        side_plan((pool2.at[f, 0], rd2.at[f]), (pool2.at[f, 1], ru2.at[f]), se2.at[f], hs2.at[f])
+        side_plan((su2.at[f], rd2.at[f]), (sd2.at[f], ru2.at[f]), se2.at[f], hs2.at[f])
         for f in range(2)
     ]
-    plan3 = side_plan((d3.at[0], rd3), (d3.at[1], ru3), se3, hs3)
+    plan3 = side_plan((su3, rd3), (sd3, ru3), se3, hs3)
     plan4 = side_plan((d2.at[pl.ds(2, 2)], d2.at[pl.ds(10, 2)]), (d2.at[pl.ds(8, 2)], d2.at[pl.ds(0, 2)]), se4, hs4)
     plan5 = side_plan((d1.at[0], rd5), (d1.at[15], ru5), se5, hs5)
 
-    for f, img in enumerate((img0, img1)):
+    lane8 = lanes((8, 128))
+    for f in range(2):
+        loads[f].wait()
         for c in range(3):
-            v = ((img[c] - OFFSETS[c]) * (1.0 / SPREADS[c])).astype(BF)
-            pf[3 * f + c, 8:72, :] = v.astype(F32)
-            edge = jnp.where(
-                lanes((64, 128)) < 4, v[:, :128].astype(F32), roll(v[:, 896:].astype(F32), 8)
-            )
-            se0[f * 192 + 64 * c : f * 192 + 64 * c + 64, :] = edge.astype(BF)
+            v = ((img[f, c] - OFFSETS[c]) * (1.0 / SPREADS[c])).astype(BF).astype(F32)
+            pf[3 * f + c, 8:72, :] = v
+    for c in range(3):
+        acc = jnp.zeros((8, 128), F32)
+        for f in range(2):
+            for y in range(8):
+                row = pf[3 * f + c, 8 + 8 * y : 16 + 8 * y, :]
+                to = 64 * f + 8 * y
+                acc = jnp.where((lane8 >= to) & (lane8 < to + 4), roll(row[:, :128], to), acc)
+                acc = jnp.where((lane8 >= to + 4) & (lane8 < to + 8), roll(row[:, 896:], to + 8), acc)
+        se0[8 * c : 8 * c + 8, :] = acc
     for buf, edge, at in ((su0, seu, 8), (sd0, sed, 68)):
         tmp[...] = jnp.zeros(tmp.shape, F32)
         for f in range(2):
@@ -188,20 +212,65 @@
     barrier_wait()
     start(0, plan0)
 
-    def shard_copy(k):
-        rows = pl.ds(i_chan * 96, 96)
+    def eye(size):
+        rows = lax.broadcasted_iota(jnp.int32, (size, size), 0)
+        return jnp.where(rows == lanes((size, size)), 1.0, 0.0).astype(BF)
+
+    def flip(one, block):
+        return lax.dot_general(
+            one, block, (((1,), (1,)), ((), ())), preferred_element_type=F32
+        ).astype(BF)
+
+    loads[2].wait()
+    own = pl.ds(pl.multiple_of(i_chan * 96, 32), 96)
+    one = eye(96)
+    for at in range(0, 1728, 256):
+        size = min(256, 1728 - at)
+        w3t[own, at : at + size] = flip(one, k3[at : at + size, :])
+
+    def shard_rows(owner, part):
+        count = 96 if part is None else 16
+        first = owner * 96 + (0 if part is None else 16 * part)
+        return w3t.at[pl.ds(pl.multiple_of(first, 16), count)]
+
+    def shard_copy(kind, part):
+        rows = shard_rows((i_chan + 2) % n_chan if kind == 2 else i_chan, part)
+        at = (0, 1, 7)[kind] + (part or 0)
         return pltpu.make_async_remote_copy(
-            src_ref=w3s,
-            dst_ref=w3t.at[rows],
-            send_sem=wsend.at[k - 1],
-            recv_sem=wrecv.at[k - 1],
-            device_id={"chan": (i_chan + k) % n_chan},
+            src_ref=rows,
+            dst_ref=rows,
+            send_sem=wsend.at[at],
+            recv_sem=wrecv.at[at],
+            device_id=far if kind == 1 else near,
             device_id_type=pl.DeviceIdType.MESH,
         )
 
-    for k in range(1, n_chan):
-        shard_copy(k).start()
-    w3t[pl.ds(pl.multiple_of(i_chan * 96, 32), 96), :] = w3s[...]
+    def shard_arrive(kind, part):
+        owner = (near["chan"], i_chan + 2, near["chan"] + 2)[kind]
+        rows = shard_rows(owner % n_chan, part)
+        at = (0, 1, 7)[kind] + (part or 0)
+        pltpu.make_async_remote_copy(
+            src_ref=rows,
+            dst_ref=rows,
+            send_sem=wsend.at[at],
+            recv_sem=wrecv.at[at],
+            device_id=far if kind == 1 else near,
+            device_id_type=pl.DeviceIdType.MESH,
+        ).wait_recv()
+
+    def shard_send(*parts):
+        if n_chan > 1:
+            for part in parts:
+                shard_copy(1, part).start()
+
+    def shard_pass(*parts):
+        if n_chan > 1:
+            for part in parts:
+                shard_arrive(1, part)
+                shard_copy(2, part).start()
+
+    if n_chan > 1:
+        shard_copy(0, None).start()
 
     for src, dst in ((b1, cb1), (b2, cb2), (b3, cb3), (l1, cl1), (l2, cl2), (l3, cl3)):
         dst[...] = jnp.transpose(jnp.broadcast_to(src[...], (128, src.shape[1])))
@@ -213,7 +282,61 @@
         want = 8 * (2 * (lane % 64) + lane // 64) + px
         sel[:, 128 * px : 128 * px + 128] = jnp.where(at == want, 1.0, 0.0).astype(BF)
 
+    loads[3].wait()
+    k1t = flip(eye(64), k1[...])
+    cell = lax.broadcasted_iota(jnp.int32, (48, 128), 0)
+    base = 48 * (cell % 4) + 16 * (cell // 16) + (cell // 4) % 4
+    lane = lanes((48, 128))
+    for cy in range(2):
+        for cx in range(2):
+            for tap in range(9):
+                want = base + (192 * (tap % 3 + cx) + 4 * (tap // 3 + cy))
+                for j in range(6):
+                    sela[48 * tap : 48 * tap + 48, 128 * j : 128 * j + 128] = jnp.where(
+                        lane + 128 * j == want, 1.0, 0.0
+                    ).astype(BF)
+            n = 2 * cy + cx
+            wb1[64 * n : 64 * n + 64, :] = dot(k1t, sela[...]).astype(BF)
+
+    kpair[...] = jnp.zeros(kpair.shape, BF)
+    half = k1[...].astype(F32)
+    both = jnp.concatenate([half, half], axis=1)
+    low = lanes((432, 128)) < 64
+    kpair[0:432, :] = jnp.where(low, both, 0.0).astype(BF)
+    kpair[512:944, :] = jnp.where(low, 0.0, both).astype(BF)
+    spot = lax.broadcasted_iota(jnp.int32, (24, 128), 0)
+    lane = lanes((24, 128))
+    in_low = (spot // 4) % 2 == 0
+    within = 16 * (spot // 8) + 4 * (spot % 4)
+    for wcy in range(4):
+        for pair in range(2):
+            for px in range(8):
+                cx, b = px // 4, px % 4
+                for side in range(2):
+                    dx = 2 - (2 * pair + side) + cx
+                    for j in range(4):
+                        hit = jnp.zeros((24, 128), F32)
+                        if 0 <= dx <= 2:
+                            for cy in range(2):
+                                dy = 2 - wcy + cy
+                                first = (dy * 3 + dx) * 48
+                                if 0 <= dy <= 2 and first < 128 * j + 128 and first + 48 > 128 * j:
+                                    match = lane + (128 * j - first - b) == within
+                                    keep_row = in_low if cy == 0 else jnp.logical_not(in_low)
+                                    hit = jnp.where(match & keep_row, 1.0, hit)
+                        bf[24 * px : 24 * px + 24, 512 * side + 128 * j : 512 * side + 128 * j + 128] = hit
+            out = dot(bf[...].astype(BF), kpair[...])
+            at = 256 * wcy + 128 * pair
+            wb1b[:, at : at + 128] = out.astype(BF)
+
+    loads[4].wait()
+    one = eye(192)
+    for at in range(0, 1600, 256):
+        size = min(256, 1600 - at)
+        w2t[:, at : at + size] = flip(one, w2n[at : at + size, :])
+
     arrive(0, plan0)
+    shard_send(0, 1)
     for buf, at in ((ru0, 4), (rd0, 72)):
         tmp[...] = buf[...].astype(F32)
         for f in range(2):
@@ -222,7 +345,9 @@
     for s, (mid, up, down) in enumerate(((rl0, 0, 2), (rr0, 1, 3))):
         for f in range(2):
             for c in range(3):
-                ef[s, 3 * f + c, 8:72, :] = mid[f * 192 + 64 * c : f * 192 + 64 * c + 64, :].astype(F32)
+                v = mid[8 * c : 8 * c + 8, :]
+                for y in range(8):
+                    ef[s, 3 * f + c, 8 + 8 * y : 16 + 8 * y, :] = roll(v, -64 * f - 8 * y)
         for corner, at in ((up, 4), (down, 72)):
             tmp[:, :128] = rc0[corner].astype(F32)
             for f in range(2):
@@ -276,30 +401,34 @@
         lax.fori_loop(0, 4, body, 0)
 
     def pack_columns(rows, side):
-        channels = side.shape[0]
-        for at in range(0, channels, 64):
-            acc = jnp.zeros((64, 128), F32)
-            lane = lanes((64, 128)) % 64
+        size = side.shape[0]
+        acc = jnp.zeros((size, 128), F32)
+        lane = lanes((size, 128)) % 64
+        for g in range(4):
             for r in range(8):
-                x = rows(r, at).astype(F32)
-                acc = jnp.where(lane == r + 2, roll(x, r + 2), acc)
-                acc = jnp.where(lane == 16 + r + 2, roll(x, 16 + r + 2 - 63), acc)
-            side[at : at + 64, :] = acc.astype(BF)
-
-    def merged(hs, at, size, step, top, bottom, base):
+                x = rows(r, slice(size * g, size * g + size)).astype(F32)
+                to = 16 * g + r
+                acc = jnp.where(lane == to, roll(x, to), acc)
+                acc = jnp.where(lane == to + 8, roll(x, to + 8 - 63), acc)
+        side[...] = acc.astype(BF)
+
+    def merged(hs):
+        size = hs.shape[1]
         lane = lanes((size, 128)) % 64
-        sides = []
-        for s, first in ((1, 0), (0, base)):
-            mid = hs[s, at : at + size, :].astype(F32)
-            up = roll(hs[2 + s, at : at + size, :].astype(F32), -step)
-            down = roll(hs[4 + s, at : at + size, :].astype(F32), step)
-            v = jnp.where(lane < first + top, up, jnp.where(lane < first + bottom, mid, down))
-            sides.append(v)
-        return jnp.where(lane < base, sides[0], sides[1])
+        slots = [hs[n].astype(F32) for n in range(6)]
+        for g in range(4):
+            v = roll(slots[1], 2 - 16 * g)
+            v = jnp.where(lane < 2, roll(slots[3], -6 - 16 * g), v)
+            v = jnp.where(lane >= 10, roll(slots[5], 10 - 16 * g), v)
+            v = jnp.where(lane >= 18, roll(slots[0], 10 - 16 * g), v)
+            v = jnp.where((lane >= 16) & (lane < 18), roll(slots[2], 2 - 16 * g), v)
+            v = jnp.where(lane >= 26, roll(slots[4], 18 - 16 * g), v)
+            hb[size * g : size * g + size, :] = v
 
     def layer_two_operand(f):
         lane = lanes((64, 128))
-        halo = merged(hs1.at[f], 0, 64, 8, 2, 10, 16)
+        merged(hs1.at[f])
+        halo = hb[0:64, :]
         for rr in range(12):
             x = pool1[f, rr].astype(F32)
             right = roll(halo, 63 - rr)
@@ -338,42 +467,67 @@
                         else:
                             pool2[f, h, rows] = jnp.where(low, keep[h, rows], mean).astype(BF)
 
-    def pack_ends(tiles, side):
-        channels = side.shape[0]
-        for at in range(0, channels, 64):
-            lane = lanes((64, 128))
-            acc = jnp.zeros((64, 128), F32)
-            for r in range(4):
-                x = tiles[r // 2, at : at + 64, :].astype(F32)
-                first = 64 * (r % 2)
-                for src, dst in ((0, r + 1), (0, 64 + r), (63, 16 + r + 1), (63, 80 + r)):
-                    acc = jnp.where(lane == dst, roll(x, dst - src - first), acc)
-            side[at : at + 64, :] = acc.astype(BF)
-
-    def merged_ends(hs, at):
-        lane = lanes((64, 128))
-        sides = []
-        for s, first in ((1, 0), (0, 16)):
-            mid = hs[s, at : at + 64, :].astype(F32)
-            up = roll(hs[2 + s, at : at + 64, :].astype(F32), -4)
-            down = roll(hs[4 + s, at : at + 64, :].astype(F32), 4)
-            v = jnp.where(lane == first, up, jnp.where(lane == first + 5, down, mid))
-            sides.append(jnp.where(lane == 64 + first + 4, down, v))
-        return jnp.where(lane % 64 < 16, sides[0], sides[1])
+    def pack_ends(tiles, side, up, down):
+        size = side.shape[0]
+        lane = lanes((size, 128))
+        acc = jnp.zeros((size, 128), F32)
+        for g in range(12):
+            for t in range(2):
+                x = tiles[t, size * g : size * g + size, :].astype(F32)
+                for r in (2 * t, 2 * t + 1):
+                    first = 64 * (r % 2)
+                    to = 8 * g + r
+                    acc = jnp.where(lane == to, roll(x, to - first), acc)
+                    acc = jnp.where(lane == to + 4, roll(x, to + 4 - 63 - first), acc)
+        side[...] = acc.astype(BF)
+        half = up.shape[0]
+        for at in range(0, half, 96):
+            rows, others = slice(at, at + 96), slice(half + at, half + at + 96)
+            low = lanes((96, 128)) < 64
+            up[rows] = jnp.where(
+                low, tiles[0, rows].astype(F32), roll(tiles[0, others].astype(F32), 64)
+            ).astype(BF)
+            down[rows] = jnp.where(
+                low, roll(tiles[1, rows].astype(F32), 64), tiles[1, others].astype(F32)
+            ).astype(BF)
+
+    def merged_ends(hs):
+        size = hs.shape[1]
+        lane = lanes((size, 128))
+        slots = [hs[n].astype(F32) for n in range(6)]
+        for g in range(12):
+            v = None
+            for first, (mid, up, down), skip in ((0, (1, 3, 5), 0), (16, (0, 2, 4), 4)):
+                to = first - 8 * g - skip
+                w = roll(slots[mid], to + 1)
+                w = jnp.where(lane == first, roll(slots[up], to - 3), w)
+                w = jnp.where(lane == first + 5, roll(slots[down], to + 5), w)
+                w = jnp.where(lane >= 64, roll(slots[mid], to + 64), w)
+                w = jnp.where(lane == first + 68, roll(slots[down], to + 68), w)
+                v = w if v is None else jnp.where(lane % 64 < 16, v, w)
+            hb[size * g : size * g + size, :] = v
 
     def layer_three_operand(tiles, from_up, from_down, hs, dst):
         channels = tiles.shape[1]
-        for at in range(0, channels, 64):
-            rows = slice(at, at + 64)
-            lane = lanes((64, 128))
+        half = channels // 2
+        merged_ends(hs)
+        for at in range(0, channels, 96):
+            rows = slice(at, at + 96)
+            fold = slice(at % half, at % half + 96)
+            lane = lanes((96, 128))
             low = lane < 64
-            halo = merged_ends(hs, at)
+            halo = hb[rows, :]
             b = tiles[0, rows].astype(F32)
             d = tiles[1, rows].astype(F32)
             b_swap, d_swap = roll(b, 64), roll(d, 64)
-            a = jnp.where(low, roll(from_up[rows].astype(F32), 64), b_swap)
+            above, below = from_up[fold].astype(F32), from_down[fold].astype(F32)
+            if at < half:
+                below = roll(below, 64)
+            else:
+                above = roll(above, 64)
+            a = jnp.where(low, above, b_swap)
             c = jnp.where(low, b_swap, d_swap)
-            e = jnp.where(low, d_swap, roll(from_down[rows].astype(F32), 64))
+            e = jnp.where(low, d_swap, below)
             for rr, (x, spots) in enumerate(
                 ((a, ((0, 0),)), (b, ((1, 0),)), (c, ((0, 1), (2, 0))), (d, ((1, 1),)), (e, ((2, 1),)))
             ):
@@ -381,9 +535,9 @@
                 right = jnp.where(lane % 64 == 63, roll(halo, 63 - rr), roll(x, 127))
                 for dx, v in enumerate((left, x, right)):
                     v = v.astype(BF)
-                    for dy, half in spots:
+                    for dy, spot in spots:
                         base = (dy * 3 + dx) * channels + at
-                        dst[base : base + 64, 128 * half : 128 * half + 128] = v
+                        dst[base : base + 96, 128 * spot : 128 * spot + 128] = v
 
     def layer_three(f):
         out = dot(w3t[...], x3[f])
@@ -424,16 +578,21 @@
     for f in range(2):
         pixels(f)
         layer_one(f)
-        pack_columns(lambda r, at: pool1[f, 2 + r], se1.at[f])
+        pack_columns(lambda r, rows: pool1[f, 2 + r, rows], se1.at[f])
         start(1 + f, plan1[f])
+        shard_send(2 + 2 * f, 3 + 2 * f)
     for f in range(2):
+        shard_pass(2 * f, 2 * f + 1)
         arrive(1 + f, plan1[f])
         layer_two_operand(f)
         layer_two(f)
-        pack_ends(pool2.at[f], se2.at[f])
+        pack_ends(pool2.at[f], se2.at[f], su2.at[f], sd2.at[f])
         start(3 + f, plan2[f])
-    for k in range(1, n_chan):
-        shard_copy(k).wait_recv()
+    shard_pass(4, 5)
+    if n_chan > 1:
+        shard_arrive(0, None)
+        for part in range(6):
+            shard_arrive(2, part)
     for f in range(2):
         arrive(3 + f, plan2[f])
         layer_three_operand(pool2.at[f], ru2.at[f], rd2.at[f], hs2.at[f], x3.at[f])
@@ -447,7 +606,7 @@
             d3[h, rows] = (dfeat * sl3[h, rows]).astype(BF)
 
         local_terms(f3, h, cl3, 256.0, pixel_count // 256, finish_three)
-    pack_ends(d3, se3)
+    pack_ends(d3, se3, su3, sd3)
     start(5, plan3)
 
     def terms_two(n, _):
@@ -458,15 +617,6 @@
         return 0
 
     lax.fori_loop(0, 8, terms_two, 0)
-
-    def terms_one(n, _):
-        def finish_one(k, rows, dfeat):
-            f1[0, n, rows] = dfeat
-
-        local_terms(f1, n, cl1, 16.0, pixel_count // 16, finish_one)
-        return 0
-
-    lax.fori_loop(0, 32, terms_one, 0)
 
     def loss_copy(axis, k):
         which = ("col", "chan", "row").index(axis)
@@ -493,16 +643,10 @@
             total = total + slots[k - 1]
         la[...] = total
 
-    loss_start("col", n_col)
-    eye = jnp.where(
-        lax.broadcasted_iota(jnp.int32, (128, 128), 0) == lanes((128, 128)), 1.0, 0.0
-    ).astype(BF)
+    one = eye(128)
     for at in range(0, 1728, 128):
         size = min(128, 1728 - at)
-        part = lax.dot_general(
-            eye[:size, :size], w3t[:, at : at + size], (((1,), (1,)), ((), ())), preferred_element_type=F32
-        )
-        w3n[at : at + size, :] = part.astype(BF)
+        w3n[at : at + size, :] = flip(one[:size, :size], w3t[:, at : at + size])
 
     arrive(5, plan3)
     layer_three_operand(d3, ru3, rd3, hs3, x3d)
@@ -511,8 +655,6 @@
         part = dot(w3n[192 * (8 - tap) : 192 * (8 - tap) + 192, :], x3d[384 * tap : 384 * tap + 384, :])
         acc = part if acc is None else acc + part
     dp2[...] = acc
-    loss_finish("col", n_col, lsa)
-    loss_start("chan", n_chan)
 
     for r in range(8):
         for k in range(3):
@@ -522,8 +664,19 @@
             swap = roll(t, 64)
             wide = jnp.where(low, t, swap) if (r // 2) % 2 == 0 else jnp.where(low, swap, t)
             d2[2 + r, rows] = ((f2[0, r, rows] + 0.25 * wide) * sl2[r, rows]).astype(BF)
-    pack_columns(lambda r, at: d2[2 + r, at : at + 64], se4)
+    pack_columns(lambda r, rows: d2[2 + r, rows], se4)
     start(6, plan4)
+
+    def terms_one(n, _):
+        def finish_one(k, rows, dfeat):
+            f1[0, n, rows] = dfeat
+
+        local_terms(f1, n, cl1, 16.0, pixel_count // 16, finish_one)
+        return 0
+
+    lax.fori_loop(0, 32, terms_one, 0)
+
+    loss_start("col", n_col)
     arrive(6, plan4)
     for rr in range(12):
         v = d2[rr]
@@ -531,8 +684,9 @@
             x4[192 * rr : 192 * rr + 192, :128] = v
         if rr >= 4:
             x4[192 * (rr - 4) : 192 * (rr - 4) + 192, 128:] = v
+    merged(hs4)
     for at in range(0, 192, 64):
-        halo = merged(hs4, at, 64, 8, 2, 10, 16)
+        halo = hb[at : at + 64, :]
         for dy in range(5):
             xh[192 * dy + at : 192 * dy + at + 64, :] = roll(halo, -dy).astype(BF)
     acc = None
@@ -540,8 +694,8 @@
         part = dot(w2n[320 * (4 - dy) : 320 * (4 - dy) + 320, :], xh[192 * dy : 192 * dy + 192, :])
         acc = part if acc is None else acc + part
     yh[...] = acc
-    loss_finish("chan", n_chan, lsb)
-    loss_start("row", n_row)
+    loss_finish("col", n_col, lsa)
+    loss_start("chan", n_chan)
     lane = lanes((64, 128))
     for i in range(4):
         acc = None
@@ -571,20 +725,29 @@
                     n = 4 * r + 2 * py + px
                     d1[2 * r + py, 64 * px : 64 * px + 64] = ((f1[0, n] + total) * sl1[n]).astype(BF)
 
-    acc = jnp.zeros((64, 128), F32)
-    for cr in range(16):
-        acc = jnp.where(lane == cr + 1, roll(d1[cr, :64].astype(F32), cr + 1), acc)
-        acc = jnp.where(lane == cr + 33, roll(d1[cr, 64:].astype(F32), cr + 33 - 127), acc)
+    lane16 = lanes((16, 128))
+    acc = jnp.zeros((16, 128), F32)
+    for g in range(4):
+        for cr in range(16):
+            to = 32 * g + cr
+            zero, one = d1[cr, 16 * g : 16 * g + 16], d1[cr, 64 + 16 * g : 80 + 16 * g]
+            acc = jnp.where(lane16 == to, roll(zero.astype(F32), to), acc)
+            acc = jnp.where(lane16 == to + 16, roll(one.astype(F32), to + 16 - 127), acc)
     se5[...] = acc.astype(BF)
     start(7, plan5)
+    loss_finish("chan", n_chan, lsb)
+    loss_start("row", n_row)
     arrive(7, plan5)
-    sides = []
-    for s, first in ((1, 0), (0, 32)):
-        mid = hs5[s].astype(F32)
-        up = roll(hs5[2 + s].astype(F32), -16)
-        down = roll(hs5[4 + s].astype(F32), 16)
-        sides.append(jnp.where(lane == first, up, jnp.where(lane == first + 17, down, mid)))
-    halo = jnp.where(lane < 32, sides[0], sides[1])
+    slots = [hs5[n].astype(F32) for n in range(6)]
+    for g in range(4):
+        v = roll(slots[1], 1 - 32 * g)
+        v = jnp.where(lane16 == 0, roll(slots[3], -15 - 32 * g), v)
+        v = jnp.where(lane16 == 17, roll(slots[5], 17 - 32 * g), v)
+        w = roll(slots[0], 17 - 32 * g)
+        w = jnp.where(lane16 == 32, roll(slots[2], 1 - 32 * g), w)
+        w = jnp.where(lane16 == 49, roll(slots[4], 33 - 32 * g), w)
+        hb[16 * g : 16 * g + 16, :] = jnp.where(lane16 < 32, v, w)
+    halo = hb[0:64, :]
     for n in range(18):
         src = ru5 if n == 0 else rd5 if n == 17 else d1.at[n - 1]
         zero, one = src[:64], src[64:]
@@ -612,7 +775,7 @@
         cols = slice(256 * part, 256 * part + 256)
         out = lax.dot_general(planes, sel[cols, :], (((1,), (1,)), ((), ())), preferred_element_type=F32)
         for c in range(3):
-            grad[c, :, cols] = out[64 * c : 64 * c + 64] * (1.0 / SPREADS[c])
+            grad[c, :, cols] = out[64 * c : 64 * c + 64].astype(BF)
 
     drain(0, plan0)
     for f in range(2):
@@ -621,22 +784,11 @@
     drain(5, plan3)
     drain(6, plan4)
     drain(7, plan5)
-    for k in range(1, n_chan):
-        shard_copy(k).wait_send()
-
-
-def block_kernel(kernel_one, flip):
-    base = kernel_one.reshape(3, 3, 3, 4, 4, 64)
-    if flip:
-        base = base[::-1, ::-1]
-    rows = []
-    for cy in range(2):
-        rows.append(
-            jnp.stack(
-                [jnp.pad(base, ((cy, 1 - cy), (cx, 1 - cx)) + ((0, 0),) * 4) for cx in range(2)]
-            )
-        )
-    return jnp.stack(rows)
+    if n_chan > 1:
+        shard_copy(0, None).wait_send()
+        for part in range(6):
+            shard_copy(1, part).wait_send()
+            shard_copy(2, part).wait_send()
 
 
 def local(
@@ -644,13 +796,12 @@
     lin_first, lin_second, lin_third,
 ):
     n_row, n_col, n_chan = lax.axis_size("row"), lax.axis_size("col"), lax.axis_size("chan")
-    wb1 = block_kernel(kernel_one, False).transpose(0, 1, 7, 3, 6, 4, 2, 5).reshape(256, 768)
-    wb1b = block_kernel(kernel_one, True).transpose(1, 6, 4, 0, 5, 2, 3, 7).reshape(192, 1024)
-    w2n = kernel_two.reshape(1600, 192)
-    w3s = kernel_three.reshape(1728, 96).T
     rows = [v.reshape(1, -1) for v in (bias_one, bias_two, bias_three, lin_first, lin_second, lin_third)]
     V = pltpu.VMEM
     scratch = dict(
+        img=V((2, 3, 64, 1024), F32), k1=V((432, 64), BF), w2n=V((1600, 192), BF), k3=V((1728, 96), BF),
+        kpair=V((1024, 128), BF), sela=V((432, 768), BF), wb1=V((256, 768), BF), wb1b=V((192, 1024), BF),
+        w2t=V((192, 1600), BF),
         sel=V((1024, 1024), BF), pf=V((6, 80, 1024), F32), ef=V((2, 6, 80, 128), F32),
         tmp=V((32, 1024), F32), lw=V((384, 1024), BF), ew=V((2, 384, 128), F32),
         x1=V((4, 768, 256), BF), f1=V((2, 32, 64, 128), F32), sl1=V((32, 64, 128), F32),
@@ -660,38 +811,45 @@
         d3=V((2, 384, 128), BF), x3d=V((3456, 256), BF), w3t=V((384, 1728), BF), w3n=V((1728, 384), BF),
         dp2=V((192, 256), F32), d2=V((12, 192, 128), BF), x4=V((1536, 256), BF), yb=V((320, 256), F32),
         xh=V((960, 128), BF), yh=V((320, 128), F32), d1=V((16, 128, 128), BF), x5=V((2560, 256), BF),
-        bf=V((192, 1024), F32), cb1=V((64, 128), F32), cb2=V((192, 128), F32), cb3=V((384, 128), F32),
+        bf=V((192, 1024), F32), hb=V((384, 128), F32), cb1=V((64, 128), F32), cb2=V((192, 128), F32), cb3=V((384, 128), F32),
         cl1=V((64, 128), F32), cl2=V((192, 128), F32), cl3=V((384, 128), F32), la=V((8, 128), F32),
         lsa=V((max(n_col - 1, 1), 8, 128), F32), lsb=V((max(n_chan - 1, 1), 8, 128), F32),
         lsc=V((max(n_row - 1, 1), 8, 128), F32),
-        su0=V((32, 1024), BF), sd0=V((32, 1024), BF), se0=V((384, 128), BF), seu=V((32, 128), BF),
-        sed=V((32, 128), BF), ru0=V((32, 1024), BF), rd0=V((32, 1024), BF), rl0=V((384, 128), BF),
-        rr0=V((384, 128), BF), rc0=V((4, 32, 128), BF),
-        se1=V((2, 64, 128), BF), hs1=V((2, 6, 64, 128), BF), se2=V((2, 192, 128), BF),
-        hs2=V((2, 6, 192, 128), BF), ru2=V((2, 192, 128), BF), rd2=V((2, 192, 128), BF),
-        se3=V((384, 128), BF), hs3=V((6, 384, 128), BF), ru3=V((384, 128), BF), rd3=V((384, 128), BF),
-        se4=V((192, 128), BF), hs4=V((6, 192, 128), BF), se5=V((64, 128), BF), hs5=V((6, 64, 128), BF),
+        su0=V((32, 1024), BF), sd0=V((32, 1024), BF), se0=V((24, 128), F32), seu=V((32, 128), BF),
+        sed=V((32, 128), BF), ru0=V((32, 1024), BF), rd0=V((32, 1024), BF), rl0=V((24, 128), F32),
+        rr0=V((24, 128), F32), rc0=V((4, 32, 128), BF),
+        se1=V((2, 16, 128), BF), hs1=V((2, 6, 16, 128), BF), se2=V((2, 16, 128), BF),
+        hs2=V((2, 6, 16, 128), BF), su2=V((2, 96, 128), BF), sd2=V((2, 96, 128), BF),
+        ru2=V((2, 96, 128), BF), rd2=V((2, 96, 128), BF),
+        se3=V((32, 128), BF), hs3=V((6, 32, 128), BF), su3=V((192, 128), BF), sd3=V((192, 128), BF),
+        ru3=V((192, 128), BF), rd3=V((192, 128), BF),
+        se4=V((48, 128), BF), hs4=V((6, 48, 128), BF), se5=V((16, 128), BF), hs5=V((6, 16, 128), BF),
         ru5=V((128, 128), BF), rd5=V((128, 128), BF),
         send_sem=pltpu.SemaphoreType.DMA((STAGES, 8)), recv_sem=pltpu.SemaphoreType.DMA((STAGES, 8)),
-        wsend=pltpu.SemaphoreType.DMA((n_chan,)), wrecv=pltpu.SemaphoreType.DMA((n_chan,)),
+        wsend=pltpu.SemaphoreType.DMA((13,)), wrecv=pltpu.SemaphoreType.DMA((13,)),
         lsend=pltpu.SemaphoreType.DMA((3, 8)), lrecv=pltpu.SemaphoreType.DMA((3, 8)),
+        in_sem=pltpu.SemaphoreType.DMA((5,)),
     )
     vmem = pl.BlockSpec(memory_space=pltpu.VMEM)
     grad, loss = pl.pallas_call(
         kernel,
         out_shape=(
-            jax.ShapeDtypeStruct(image_gen.shape, F32),
+            jax.ShapeDtypeStruct(image_gen.shape, BF),
             jax.ShapeDtypeStruct((1, 1), F32),
         ),
-        in_specs=[vmem] * 13,
+        in_specs=[pl.BlockSpec(memory_space=pl.ANY)] * 5 + [vmem] * 6,
         out_specs=(vmem, vmem),
         scratch_shapes=list(scratch.values()),
         compiler_params=pltpu.CompilerParams(
             collective_id=0, has_side_effects=True, vmem_limit_bytes=62 * 1024 * 1024
         ),
         name="whole",
-    )(image_gen, image_ref, wb1, w2n.T, w2n, w3s, wb1b, *rows)
-    return (grad, loss.reshape(()))
+    )(
+        image_gen, image_ref, kernel_one.reshape(432, 64), kernel_two.reshape(1600, 192),
+        kernel_three.reshape(1728, 96), *rows,
+    )
+    spreads = jnp.array(SPREADS, F32)[:, None, None]
+    return (grad.astype(F32) / spreads, loss.reshape(()))
 
 
 def solution(mesh):

time: 92.6 us -> 59.4 us (0.64)
  the two profiles are of different devices: /device:TPU:25 before, /device:TPU:1 now
where the time goes in v1:
time: 59.4 us; the launch traced here: 59.1 us
  Pallas kernels  52 us (88%)
  local copies, waits for them, and re-layouts  2.59 us (4%)
  between operations  2.47 us (4%)
  other arithmetic  2.03 us (3%)
    pallas_call x1, Pallas kernels, local(): pl.pallas_call(kernel, out_shape=(jax.ShapeDtypeStruct(image_gen.shape, B...  52 us
    div x1, other arithmetic, local(): return (grad.astype(F32) / spreads, loss.reshape(()))  2.03 us
    unnamed x6, local copies, waits for them, and re-layouts  1.44 us

profile of v1, /device:TPU:1, one launch (start us, length us, event | category | flops | bytes accessed | tf_op | source)
XLA Modules:
  0.0 59.1 jit_solution(7381856246433682755)
XLA Ops:
  0.6 0.0 copy-start
  0.6 0.7 %copy-done = f32[384]{0:T(512)S(1)} copy-done((f32[384]{0:T(512)S(1)}, f32[384]{0:T(512)}, u32[]{:S(2)}) %copy-start) | copy-done | bytes 1560
  1.3 0.0 copy-start.1
  1.3 0.6 reshape.40.b3
  1.9 0.1 copy-done.1
  2.0 0.6 reshape.43.l3
  2.6 52.0 %whole.1 = (bf16[3,64,1024]{2,1,0:T(8,128)(2,1)}, f32[1,1]{1,0:T(1,128)}) custom-call(f32[3,64,1024]{2,1,0:T(8,128)} %img0_hbm.1, f32[3,64,1024]{2,1,0:T(8,128)} %img1_hbm.1, bf16[432,64]{1,0:T(8,128)(2,1)} %bitcast.10, bf16[1600,192]{1,0:T(8,128)(2,1)} %bitcast.8, bf16[1728,96]{1,0:T(8,128)(2,1)} %bitcast.9, f32[1,64]{1,0:T(1,128)} %bitcast.13, ...), custom_call_target="tpu_custom_call" | custom-call | tf_op jit(solution)/shard_map/whole/pallas_call | solution.py:834
  54.6 0.0 copy-start.2
  54.6 0.6 %copy-done.2 = f32[3]{0:T(128)S(1)} copy-done((f32[3]{0:T(128)S(1)}, f32[3]{0:T(128)}, u32[]{:S(2)}) %copy-start.2) | copy-done | bytes 36
  55.2 2.0 %convert_multiply_fusion = f32[3,64,1024]{2,1,0:T(8,128)} fusion(bf16[3,64,1024]{2,1,0:T(8,128)(2,1)} %get-tuple-element.4, f32[3]{0:T(128)S(1)} %copy-done.2), kind=kLoop, calls=%fused_computation | loop fusion | flops 393216 | bytes 1179660 | tf_op jit(solution)/shard_map/div | solution.py:852
Async XLA Ops:
  0.6 0.7 %copy-start = (f32[384]{0:T(512)S(1)}, f32[384]{0:T(512)}, u32[]{:S(2)}) copy-start(f32[384]{0:T(512)} %param.19) | copy-start | bytes 4612
  1.3 0.7 %copy-start.1 = (f32[384]{0:T(512)S(1)}, f32[384]{0:T(512)}, u32[]{:S(2)}) copy-start(f32[384]{0:T(512)} %param.22) | copy-start | bytes 4612
  54.6 0.7 %copy-start.2 = (f32[3]{0:T(128)S(1)}, f32[3]{0:T(128)}, u32[]{:S(2)}) copy-start(f32[3]{0:T(128)} %constant.3) | copy-start | bytes 40

commit v2 on v1

--- a/solution.py
+++ b/solution.py
@@ -41,10 +41,10 @@
 
 def kernel(
     img0_hbm, img1_hbm, k1_hbm, k2_hbm, k3_hbm, b1, b2, b3, l1, l2, l3,
-    grad, loss,
+    planes, loss,
     img, k1, w2n, k3, kpair, sela, wb1, wb1b, w2t,
     sel, pf, ef, tmp, lw, ew, x1, f1, sl1, pool1, x2, f2, sl2, keep, pool2, x3,
-    f3, sl3, d3, x3d, w3t, w3n, dp2, d2, x4, yb, xh, yh, d1, x5, bf, hb,
+    f3, sl3, d3, x3d, w3t, w3n, dp2, d2, x4, yb, xh, yh, d1, x5, bf, hb, wends, dp1, xe,
     cb1, cb2, cb3, cl1, cl2, cl3, la, lsa, lsb, lsc,
     su0, sd0, se0, seu, sed, ru0, rd0, rl0, rr0, rc0,
     se1, hs1, se2, hs2, su2, sd2, ru2, rd2, se3, hs3, su3, sd3, ru3, rd3, se4, hs4, se5, hs5, ru5, rd5,
@@ -273,7 +273,7 @@
         shard_copy(0, None).start()
 
     for src, dst in ((b1, cb1), (b2, cb2), (b3, cb3), (l1, cl1), (l2, cl2), (l3, cl3)):
-        dst[...] = jnp.transpose(jnp.broadcast_to(src[...], (128, src.shape[1])))
+        dst[...] = jnp.transpose(jnp.broadcast_to(src[...].reshape(1, -1), (128, src.shape[0])))
     la[...] = jnp.zeros(la.shape, F32)
 
     for px in range(8):
@@ -297,37 +297,6 @@
                     ).astype(BF)
             n = 2 * cy + cx
             wb1[64 * n : 64 * n + 64, :] = dot(k1t, sela[...]).astype(BF)
-
-    kpair[...] = jnp.zeros(kpair.shape, BF)
-    half = k1[...].astype(F32)
-    both = jnp.concatenate([half, half], axis=1)
-    low = lanes((432, 128)) < 64
-    kpair[0:432, :] = jnp.where(low, both, 0.0).astype(BF)
-    kpair[512:944, :] = jnp.where(low, 0.0, both).astype(BF)
-    spot = lax.broadcasted_iota(jnp.int32, (24, 128), 0)
-    lane = lanes((24, 128))
-    in_low = (spot // 4) % 2 == 0
-    within = 16 * (spot // 8) + 4 * (spot % 4)
-    for wcy in range(4):
-        for pair in range(2):
-            for px in range(8):
-                cx, b = px // 4, px % 4
-                for side in range(2):
-                    dx = 2 - (2 * pair + side) + cx
-                    for j in range(4):
-                        hit = jnp.zeros((24, 128), F32)
-                        if 0 <= dx <= 2:
-                            for cy in range(2):
-                                dy = 2 - wcy + cy
-                                first = (dy * 3 + dx) * 48
-                                if 0 <= dy <= 2 and first < 128 * j + 128 and first + 48 > 128 * j:
-                                    match = lane + (128 * j - first - b) == within
-                                    keep_row = in_low if cy == 0 else jnp.logical_not(in_low)
-                                    hit = jnp.where(match & keep_row, 1.0, hit)
-                        bf[24 * px : 24 * px + 24, 512 * side + 128 * j : 512 * side + 128 * j + 128] = hit
-            out = dot(bf[...].astype(BF), kpair[...])
-            at = 256 * wcy + 128 * pair
-            wb1b[:, at : at + 128] = out.astype(BF)
 
     loads[4].wait()
     one = eye(192)
@@ -581,6 +550,43 @@
         pack_columns(lambda r, rows: pool1[f, 2 + r, rows], se1.at[f])
         start(1 + f, plan1[f])
         shard_send(2 + 2 * f, 3 + 2 * f)
+    kpair[...] = jnp.zeros(kpair.shape, BF)
+    half = k1[...].astype(F32)
+    both = jnp.concatenate([half, half], axis=1)
+    low = lanes((432, 128)) < 64
+    kpair[0:432, :] = jnp.where(low, both, 0.0).astype(BF)
+    kpair[512:944, :] = jnp.where(low, 0.0, both).astype(BF)
+    spot = lax.broadcasted_iota(jnp.int32, (24, 128), 0)
+    lane = lanes((24, 128))
+    in_low = (spot // 4) % 2 == 0
+    within = 16 * (spot // 8) + 4 * (spot % 4)
+    for wcy in range(4):
+        for pair in range(2):
+            for px in range(8):
+                cx, b = px // 4, px % 4
+                for side in range(2):
+                    dx = 2 - (2 * pair + side) + cx
+                    for j in range(4):
+                        hit = jnp.zeros((24, 128), F32)
+                        if 0 <= dx <= 2:
+                            for cy in range(2):
+                                dy = 2 - wcy + cy
+                                first = (dy * 3 + dx) * 48
+                                if 0 <= dy <= 2 and first < 128 * j + 128 and first + 48 > 128 * j:
+                                    match = lane + (128 * j - first - b) == within
+                                    keep_row = in_low if cy == 0 else jnp.logical_not(in_low)
+                                    hit = jnp.where(match & keep_row, 1.0, hit)
+                        bf[24 * px : 24 * px + 24, 512 * side + 128 * j : 512 * side + 128 * j + 128] = hit
+            out = dot(bf[...].astype(BF), kpair[...])
+            at = 256 * wcy + 128 * pair
+            wb1b[:, at : at + 128] = out.astype(BF)
+
+    for side in range(2):
+        at = 96 * side
+        wends[side] = jnp.concatenate(
+            [wb1b[at : at + 96, 256 * w + 192 * side : 256 * w + 192 * side + 64].astype(F32) for w in range(4)], axis=1
+        ).astype(BF)
+
     for f in range(2):
         shard_pass(2 * f, 2 * f + 1)
         arrive(1 + f, plan1[f])
@@ -589,6 +595,26 @@
         pack_ends(pool2.at[f], se2.at[f], su2.at[f], sd2.at[f])
         start(3 + f, plan2[f])
     shard_pass(4, 5)
+    pixel_count = 64 * n_tile * 1024 * n_col
+
+    def terms_two(n, _):
+        def finish_two(k, rows, dfeat):
+            f2[0, n, rows] = dfeat
+
+        local_terms(f2, n, cl2, 64.0, pixel_count // 64, finish_two)
+        return 0
+
+    lax.fori_loop(0, 8, terms_two, 0)
+
+    def terms_one(n, _):
+        def finish_one(k, rows, dfeat):
+            f1[0, n, rows] = dfeat
+
+        local_terms(f1, n, cl1, 16.0, pixel_count // 16, finish_one)
+        return 0
+
+    lax.fori_loop(0, 32, terms_one, 0)
+
     if n_chan > 1:
         shard_arrive(0, None)
         for part in range(6):
@@ -597,26 +623,6 @@
         arrive(3 + f, plan2[f])
         layer_three_operand(pool2.at[f], ru2.at[f], rd2.at[f], hs2.at[f], x3.at[f])
         layer_three(f)
-
-    pixel_count = 64 * n_tile * 1024 * n_col
-
-    for h in range(2):
-
-        def finish_three(k, rows, dfeat):
-            d3[h, rows] = (dfeat * sl3[h, rows]).astype(BF)
-
-        local_terms(f3, h, cl3, 256.0, pixel_count // 256, finish_three)
-    pack_ends(d3, se3, su3, sd3)
-    start(5, plan3)
-
-    def terms_two(n, _):
-        def finish_two(k, rows, dfeat):
-            f2[0, n, rows] = dfeat
-
-        local_terms(f2, n, cl2, 64.0, pixel_count // 64, finish_two)
-        return 0
-
-    lax.fori_loop(0, 8, terms_two, 0)
 
     def loss_copy(axis, k):
         which = ("col", "chan", "row").index(axis)
@@ -643,12 +649,25 @@
             total = total + slots[k - 1]
         la[...] = total
 
+    for h in range(2):
+
+        def finish_three(k, rows, dfeat):
+            d3[h, rows] = (dfeat * sl3[h, rows]).astype(BF)
+
+        local_terms(f3, h, cl3, 256.0, pixel_count // 256, finish_three)
+    pack_ends(d3, se3, su3, sd3)
+    start(5, plan3)
+    loss_start("col", n_col)
+
+
     one = eye(128)
     for at in range(0, 1728, 128):
         size = min(128, 1728 - at)
         w3n[at : at + size, :] = flip(one[:size, :size], w3t[:, at : at + size])
 
     arrive(5, plan3)
+    loss_finish("col", n_col, lsa)
+    loss_start("chan", n_chan)
     layer_three_operand(d3, ru3, rd3, hs3, x3d)
     acc = None
     for tap in range(9):
@@ -667,63 +686,67 @@
     pack_columns(lambda r, rows: d2[2 + r, rows], se4)
     start(6, plan4)
 
-    def terms_one(n, _):
-        def finish_one(k, rows, dfeat):
-            f1[0, n, rows] = dfeat
-
-        local_terms(f1, n, cl1, 16.0, pixel_count // 16, finish_one)
-        return 0
-
-    lax.fori_loop(0, 32, terms_one, 0)
-
-    loss_start("col", n_col)
-    arrive(6, plan4)
+    zero = jnp.zeros((192, 128), BF)
     for rr in range(12):
-        v = d2[rr]
+        v = d2[rr] if 2 <= rr < 10 else zero
         if rr < 8:
             x4[192 * rr : 192 * rr + 192, :128] = v
         if rr >= 4:
             x4[192 * (rr - 4) : 192 * (rr - 4) + 192, 128:] = v
+    lane = lanes((64, 128))
+
+    def joined(pick):
+        total = pick(0)
+        for e, edge in ((1, lane == 127), (-1, lane == 0), (2, lane % 64 == 63), (-2, lane % 64 == 0)):
+            total = total + jnp.where(edge, 0.0, shifted(pick(e), e))
+        return total
+
+    def taps(operand, pairs):
+        acc = None
+        for dy, block in pairs:
+            part = dot(w2n[320 * (4 - dy) : 320 * (4 - dy) + 320, :], operand(block))
+            acc = part if acc is None else acc + part
+        return acc
+
+    for i in range(4):
+        yb[...] = taps(lambda n: x4[192 * n : 192 * n + 192, :], [(dy, i + dy) for dy in range(5)])
+        for h in range(2):
+            dp1[i + 4 * h] = joined(
+                lambda e: yb[64 * (2 - e) : 64 * (2 - e) + 64, 128 * h : 128 * h + 128]
+            )
+
+    arrive(6, plan4)
+    loss_finish("chan", n_chan, lsb)
+    loss_start("row", n_row)
     merged(hs4)
     for at in range(0, 192, 64):
         halo = hb[at : at + 64, :]
         for dy in range(5):
             xh[192 * dy + at : 192 * dy + at + 64, :] = roll(halo, -dy).astype(BF)
-    acc = None
-    for dy in range(5):
-        part = dot(w2n[320 * (4 - dy) : 320 * (4 - dy) + 320, :], xh[192 * dy : 192 * dy + 192, :])
-        acc = part if acc is None else acc + part
-    yh[...] = acc
-    loss_finish("col", n_col, lsa)
-    loss_start("chan", n_chan)
-    lane = lanes((64, 128))
-    for i in range(4):
-        acc = None
-        for dy in range(5):
-            part = dot(
-                w2n[320 * (4 - dy) : 320 * (4 - dy) + 320, :],
-                x4[192 * (i + dy) : 192 * (i + dy) + 192, :],
+    yh[...] = taps(lambda n: xh[192 * n : 192 * n + 192, :], [(dy, dy) for dy in range(5)])
+    for n, v in enumerate((d2[0], d2[1], d2[1], zero, d2[10], d2[11], zero, d2[10])):
+        xe[192 * (n // 2) : 192 * (n // 2) + 192, 128 * (n % 2) : 128 * (n % 2) + 128] = v
+    for first, pairs in ((0, ((0, 0), (1, 1))), (6, ((4, 2), (3, 3)))):
+        yb[...] = taps(lambda n: xe[192 * n : 192 * n + 192, :], pairs)
+        for h in range(2):
+            dp1[first + h] = dp1[first + h] + joined(
+                lambda e: yb[64 * (2 - e) : 64 * (2 - e) + 64, 128 * h : 128 * h + 128]
             )
-            acc = part if acc is None else acc + part
-        yb[...] = acc
-        for h in range(2):
-            r = i + 4 * h
-
-            def piece(e, src=None):
-                if src is None:
-                    return yb[64 * (2 - e) : 64 * (2 - e) + 64, 128 * h : 128 * h + 128]
-                return yh[64 * (2 - e) : 64 * (2 - e) + 64, :]
-
-            total = piece(0)
-            total = total + jnp.where(lane == 127, roll(piece(1, 1), 127 - r), shifted(piece(1), 1))
-            total = total + jnp.where(lane % 64 == 63, roll(piece(2, 1), 63 - r), shifted(piece(2), 2))
-            total = total + jnp.where(lane == 0, roll(piece(-1, 1), -80 - r), shifted(piece(-1), -1))
-            total = total + jnp.where(lane % 64 == 0, roll(piece(-2, 1), -16 - r), shifted(piece(-2), -2))
-            total = 0.25 * total
-            for py in range(2):
-                for px in range(2):
-                    n = 4 * r + 2 * py + px
-                    d1[2 * r + py, 64 * px : 64 * px + 64] = ((f1[0, n] + total) * sl1[n]).astype(BF)
+    for r in range(8):
+
+        def side(e):
+            return yh[64 * (2 - e) : 64 * (2 - e) + 64, :]
+
+        total = dp1[r]
+        total = total + jnp.where(lane == 127, roll(side(1), 127 - r), 0.0)
+        total = total + jnp.where(lane % 64 == 63, roll(side(2), 63 - r), 0.0)
+        total = total + jnp.where(lane == 0, roll(side(-1), -80 - r), 0.0)
+        total = total + jnp.where(lane % 64 == 0, roll(side(-2), -16 - r), 0.0)
+        total = 0.25 * total
+        for py in range(2):
+            for px in range(2):
+                n = 4 * r + 2 * py + px
+                d1[2 * r + py, 64 * px : 64 * px + 64] = ((f1[0, n] + total) * sl1[n]).astype(BF)
 
     lane16 = lanes((16, 128))
     acc = jnp.zeros((16, 128), F32)
@@ -735,8 +758,35 @@
             acc = jnp.where(lane16 == to + 16, roll(one.astype(F32), to + 16 - 127), acc)
     se5[...] = acc.astype(BF)
     start(7, plan5)
-    loss_finish("chan", n_chan, lsb)
-    loss_start("row", n_row)
+
+    def beside(src):
+        zero, one = src[:64], src[64:]
+        before = jnp.where(lane == 0, 0.0, shifted(one.astype(F32), -1)).astype(BF)
+        after = jnp.where(lane == 127, 0.0, shifted(zero.astype(F32), 1)).astype(BF)
+        return before, zero, one, after
+
+    for n in range(18):
+        if n in (0, 17):
+            cols = (jnp.zeros((64, 128), BF),) * 4
+        else:
+            cols = beside(d1.at[n - 1])
+        for g, v in enumerate(cols):
+            if n < 10:
+                x5[256 * n + 64 * g : 256 * n + 64 * g + 64, :128] = v
+            if n >= 8:
+                x5[256 * (n - 8) + 64 * g : 256 * (n - 8) + 64 * g + 64, 128:] = v
+
+    def spots(r):
+        for px in range(8):
+            for c in range(3):
+                yield px * 24 + c * 8, 64 * c + 8 * r, 128 * px
+
+    for i in range(4):
+        out = dot(wb1b[...], x5[512 * i : 512 * i + 1024, :])
+        for h in range(2):
+            for at, row, col in spots(i + 4 * h):
+                bf[row : row + 8, col : col + 128] = out[at : at + 8, 128 * h : 128 * h + 128]
+
     arrive(7, plan5)
     slots = [hs5[n].astype(F32) for n in range(6)]
     for g in range(4):
@@ -747,35 +797,24 @@
         w = jnp.where(lane16 == 32, roll(slots[2], 1 - 32 * g), w)
         w = jnp.where(lane16 == 49, roll(slots[4], 33 - 32 * g), w)
         hb[16 * g : 16 * g + 16, :] = jnp.where(lane16 < 32, v, w)
+    for r, src, at in ((0, ru5, 0), (7, rd5, 768)):
+        out = dot(wb1b[:, at : at + 256], jnp.concatenate(beside(src), axis=0))
+        for at, row, col in spots(r):
+            bf[row : row + 8, col : col + 128] = bf[row : row + 8, col : col + 128] + out[at : at + 8]
     halo = hb[0:64, :]
-    for n in range(18):
-        src = ru5 if n == 0 else rd5 if n == 17 else d1.at[n - 1]
-        zero, one = src[:64], src[64:]
-        before = jnp.where(lane == 0, roll(halo, -32 - n), shifted(one.astype(F32), -1)).astype(BF)
-        after = jnp.where(lane == 127, roll(halo, 127 - n), shifted(zero.astype(F32), 1)).astype(BF)
-        for g, v in enumerate((before, zero, one, after)):
-            if n < 10:
-                x5[256 * n + 64 * g : 256 * n + 64 * g + 64, :128] = v
-            if n >= 8:
-                x5[256 * (n - 8) + 64 * g : 256 * (n - 8) + 64 * g + 64, 128:] = v
-    for i in range(4):
-        out = dot(wb1b[...], x5[512 * i : 512 * i + 1024, :])
-        for h in range(2):
-            r = i + 4 * h
-            for px in range(8):
-                for c in range(3):
-                    at = px * 24 + c * 8
-                    bf[64 * c + 8 * r : 64 * c + 8 * r + 8, 128 * px : 128 * px + 128] = out[
-                        at : at + 8, 128 * h : 128 * h + 128
-                    ]
+    stack = jnp.concatenate([roll(halo, -w).astype(BF) for w in range(4)], axis=0)
+    for side, (first, edge) in enumerate(((32, 0), (0, 127))):
+        yh[0:96, :] = dot(wends[side], stack)
+        for r in range(8):
+            for at, row, col in spots(r):
+                if at // 96 == side:
+                    part = roll(yh[at - 96 * side : at - 96 * side + 8, :], edge - first - 2 * r)
+                    bf[row : row + 8, col : col + 128] = bf[row : row + 8, col : col + 128] + jnp.where(
+                        lane8 == edge, part, 0.0
+                    )
     loss_finish("row", n_row, lsc)
     loss[...] = jnp.sum(la[0:1, :], axis=1, keepdims=True)
-    planes = bf[...].astype(BF)
-    for part in range(4):
-        cols = slice(256 * part, 256 * part + 256)
-        out = lax.dot_general(planes, sel[cols, :], (((1,), (1,)), ((), ())), preferred_element_type=F32)
-        for c in range(3):
-            grad[c, :, cols] = out[64 * c : 64 * c + 64].astype(BF)
+    planes[...] = bf[...].astype(BF)
 
     drain(0, plan0)
     for f in range(2):
@@ -791,12 +830,27 @@
             shard_copy(2, part).wait_send()
 
 
+def to_pixels(planes, grad, want):
+    @pl.when(pl.program_id(0) == 0)
+    def _():
+        at = lax.broadcasted_iota(jnp.int32, (1024, 128), 0)
+        want[...] = 8 * (2 * (at % 64) + (at // 64) % 2) + at // 128 - lanes((1024, 128))
+
+    first = 256 * pl.program_id(0)
+    spread = jnp.concatenate(
+        [jnp.where(want[...] == first + 128 * j, 1.0, 0.0).astype(BF) for j in range(2)], axis=1
+    )
+    out = dot(planes[...], spread)
+    for c in range(3):
+        grad[c] = out[64 * c : 64 * c + 64] * (1.0 / SPREADS[c])
+
+
 def local(
     image_gen, image_ref, kernel_one, bias_one, kernel_two, bias_two, kernel_three, bias_three,
     lin_first, lin_second, lin_third,
 ):
     n_row, n_col, n_chan = lax.axis_size("row"), lax.axis_size("col"), lax.axis_size("chan")
-    rows = [v.reshape(1, -1) for v in (bias_one, bias_two, bias_three, lin_first, lin_second, lin_third)]
+    rows = (bias_one, bias_two, bias_three, lin_first, lin_second, lin_third)
     V = pltpu.VMEM
     scratch = dict(
         img=V((2, 3, 64, 1024), F32), k1=V((432, 64), BF), w2n=V((1600, 192), BF), k3=V((1728, 96), BF),
@@ -811,7 +865,8 @@
         d3=V((2, 384, 128), BF), x3d=V((3456, 256), BF), w3t=V((384, 1728), BF), w3n=V((1728, 384), BF),
         dp2=V((192, 256), F32), d2=V((12, 192, 128), BF), x4=V((1536, 256), BF), yb=V((320, 256), F32),
         xh=V((960, 128), BF), yh=V((320, 128), F32), d1=V((16, 128, 128), BF), x5=V((2560, 256), BF),
-        bf=V((192, 1024), F32), hb=V((384, 128), F32), cb1=V((64, 128), F32), cb2=V((192, 128), F32), cb3=V((384, 128), F32),
+        bf=V((192, 1024), F32), hb=V((384, 128), F32), wends=V((2, 96, 256), BF), dp1=V((8, 64, 128), F32),
+        xe=V((768, 256), BF), cb1=V((64, 128), F32), cb2=V((192, 128), F32), cb3=V((384, 128), F32),
         cl1=V((64, 128), F32), cl2=V((192, 128), F32), cl3=V((384, 128), F32), la=V((8, 128), F32),
         lsa=V((max(n_col - 1, 1), 8, 128), F32), lsb=V((max(n_chan - 1, 1), 8, 128), F32),
         lsc=V((max(n_row - 1, 1), 8, 128), F32),
@@ -831,10 +886,10 @@
         in_sem=pltpu.SemaphoreType.DMA((5,)),
     )
     vmem = pl.BlockSpec(memory_space=pltpu.VMEM)
-    grad, loss = pl.pallas_call(
+    planes, loss = pl.pallas_call(
         kernel,
         out_shape=(
-            jax.ShapeDtypeStruct(image_gen.shape, BF),
+            jax.ShapeDtypeStruct((192, 1024), BF),
             jax.ShapeDtypeStruct((1, 1), F32),
         ),
         in_specs=[pl.BlockSpec(memory_space=pl.ANY)] * 5 + [vmem] * 6,
@@ -848,8 +903,16 @@
         image_gen, image_ref, kernel_one.reshape(432, 64), kernel_two.reshape(1600, 192),
         kernel_three.reshape(1728, 96), *rows,
     )
-    spreads = jnp.array(SPREADS, F32)[:, None, None]
-    return (grad.astype(F32) / spreads, loss.reshape(()))
+    grad = pl.pallas_call(
+        to_pixels,
+        out_shape=jax.ShapeDtypeStruct(image_gen.shape, F32),
+        grid=(4,),
+        in_specs=[pl.BlockSpec((192, 1024), lambda n: (0, 0))],
+        out_specs=pl.BlockSpec((3, 64, 256), lambda n: (0, 0, n)),
+        scratch_shapes=[pltpu.VMEM((1024, 128), jnp.int32)],
+        name="pixels",
+    )(planes)
+    return (grad, loss.reshape(()))
 
 
 def solution(mesh):

time: 59.4 us -> 54.2 us (0.912)
  the two profiles are of different devices: /device:TPU:1 before, /device:TPU:25 now
where the time goes in v2:
time: 54.2 us; the launch traced here: 54 us
  Pallas kernels  51.6 us (95%)
  between operations  2.4 us (4%)
    pallas_call x1, Pallas kernels, local(): pl.pallas_call(kernel, out_shape=(jax.ShapeDtypeStruct((192, 1024), BF),...  48.2 us
    pallas_call x1, Pallas kernels, local(): pl.pallas_call(to_pixels, out_shape=jax.ShapeDtypeStruct(image_gen.shape,...  3.39 us

profile of v2, /device:TPU:25, one launch (start us, length us, event | category | flops | bytes accessed | tf_op | source)
XLA Modules:
  0.0 54.0 jit_solution(17648097853468168094)
XLA Ops:
  0.6 48.2 %whole.1 = (bf16[192,1024]{1,0:T(8,128)(2,1)}, f32[1,1]{1,0:T(1,128)}) custom-call(f32[3,64,1024]{2,1,0:T(8,128)} %img0_hbm.1, f32[3,64,1024]{2,1,0:T(8,128)} %img1_hbm.1, bf16[432,64]{1,0:T(8,128)(2,1)} %bitcast.6, bf16[1600,192]{1,0:T(8,128)(2,1)} %bitcast.4, bf16[1728,96]{1,0:T(8,128)(2,1)} %bitcast.5, f32[64]{0:T(128)} %b1.1, f32[192]{0:T(256)} %b2.1, ...), custom_call_target="tpu_custom_call" | custom-call | tf_op jit(solution)/shard_map/whole/pallas_call | solution.py:889
  48.8 3.4 %pixels.1 = f32[3,64,1024]{2,1,0:T(8,128)} custom-call(bf16[192,1024]{1,0:T(8,128)(2,1)} %get-tuple-element.4.planes), custom_call_target="tpu_custom_call" | custom-call | tf_op jit(solution)/shard_map/pixels/pallas_call | solution.py:906

commit v3 on v2

--- a/solution.py
+++ b/solution.py
@@ -271,6 +271,7 @@
 
     if n_chan > 1:
         shard_copy(0, None).start()
+    shard_send(0, 1, 2)
 
     for src, dst in ((b1, cb1), (b2, cb2), (b3, cb3), (l1, cl1), (l2, cl2), (l3, cl3)):
         dst[...] = jnp.transpose(jnp.broadcast_to(src[...].reshape(1, -1), (128, src.shape[0])))
@@ -305,7 +306,6 @@
         w2t[:, at : at + size] = flip(one, w2n[at : at + size, :])
 
     arrive(0, plan0)
-    shard_send(0, 1)
     for buf, at in ((ru0, 4), (rd0, 72)):
         tmp[...] = buf[...].astype(F32)
         for f in range(2):
@@ -549,7 +549,7 @@
         layer_one(f)
         pack_columns(lambda r, rows: pool1[f, 2 + r, rows], se1.at[f])
         start(1 + f, plan1[f])
-        shard_send(2 + 2 * f, 3 + 2 * f)
+        shard_send(*((3, 4), (5,))[f])
     kpair[...] = jnp.zeros(kpair.shape, BF)
     half = k1[...].astype(F32)
     both = jnp.concatenate([half, half], axis=1)
@@ -665,6 +665,15 @@
         size = min(128, 1728 - at)
         w3n[at : at + size, :] = flip(one[:size, :size], w3t[:, at : at + size])
 
+    drain(0, plan0)
+    for f in range(2):
+        drain(1 + f, plan1[f])
+        drain(3 + f, plan2[f])
+    if n_chan > 1:
+        shard_copy(0, None).wait_send()
+        for part in range(6):
+            shard_copy(1, part).wait_send()
+            shard_copy(2, part).wait_send()
     arrive(5, plan3)
     loss_finish("col", n_col, lsa)
     loss_start("chan", n_chan)
@@ -715,6 +724,7 @@
                 lambda e: yb[64 * (2 - e) : 64 * (2 - e) + 64, 128 * h : 128 * h + 128]
             )
 
+    drain(5, plan3)
     arrive(6, plan4)
     loss_finish("chan", n_chan, lsb)
     loss_start("row", n_row)
@@ -787,6 +797,7 @@
             for at, row, col in spots(i + 4 * h):
                 bf[row : row + 8, col : col + 128] = out[at : at + 8, 128 * h : 128 * h + 128]
 
+    drain(6, plan4)
     arrive(7, plan5)
     slots = [hs5[n].astype(F32) for n in range(6)]
     for g in range(4):
@@ -816,18 +827,7 @@
     loss[...] = jnp.sum(la[0:1, :], axis=1, keepdims=True)
     planes[...] = bf[...].astype(BF)
 
-    drain(0, plan0)
-    for f in range(2):
-        drain(1 + f, plan1[f])
-        drain(3 + f, plan2[f])
-    drain(5, plan3)
-    drain(6, plan4)
     drain(7, plan5)
-    if n_chan > 1:
-        shard_copy(0, None).wait_send()
-        for part in range(6):
-            shard_copy(1, part).wait_send()
-            shard_copy(2, part).wait_send()
 
 
 def to_pixels(planes, grad, want):

time: 54.2 us -> 53.3 us (0.983)
  Pallas kernels: 51.6 us -> 50.7 us
    pallas_call x1, Pallas kernels: 48.2 us -> 47.3 us  [local(): pl.pallas_call(kernel, out_shape=(jax.ShapeDtypeStruct((192, 1024), BF),...]
where the time goes in v3:
time: 53.3 us; the launch traced here: 53.1 us
  Pallas kernels  50.7 us (95%)
  between operations  2.4 us (5%)
    pallas_call x1, Pallas kernels, local(): pl.pallas_call(kernel, out_shape=(jax.ShapeDtypeStruct((192, 1024), BF),...  47.3 us
    pallas_call x1, Pallas kernels, local(): pl.pallas_call(to_pixels, out_shape=jax.ShapeDtypeStruct(image_gen.shape,...  3.39 us

profile of v3, /device:TPU:25, one launch (start us, length us, event | category | flops | bytes accessed | tf_op | source)
XLA Modules:
  0.0 53.1 jit_solution(5937717412752250355)
XLA Ops:
  0.6 47.3 %whole.1 = (bf16[192,1024]{1,0:T(8,128)(2,1)}, f32[1,1]{1,0:T(1,128)}) custom-call(f32[3,64,1024]{2,1,0:T(8,128)} %img0_hbm.1, f32[3,64,1024]{2,1,0:T(8,128)} %img1_hbm.1, bf16[432,64]{1,0:T(8,128)(2,1)} %bitcast.6, bf16[1600,192]{1,0:T(8,128)(2,1)} %bitcast.4, bf16[1728,96]{1,0:T(8,128)(2,1)} %bitcast.5, f32[64]{0:T(128)} %b1.1, f32[192]{0:T(256)} %b2.1, ...), custom_call_target="tpu_custom_call" | custom-call | tf_op jit(solution)/shard_map/whole/pallas_call | solution.py:889
  47.9 3.4 %pixels.1 = f32[3,64,1024]{2,1,0:T(8,128)} custom-call(bf16[192,1024]{1,0:T(8,128)(2,1)} %get-tuple-element.4.planes), custom_call_target="tpu_custom_call" | custom-call | tf_op jit(solution)/shard_map/pixels/pallas_call | solution.py:906

commit v4 on v3

--- a/solution.py
+++ b/solution.py
@@ -147,10 +147,6 @@
             def _():
                 copy(stage, d, src, dst).wait_recv()
 
-            @pl.when(jnp.logical_not(exists(*back)))
-            def _():
-                dst[...] = jnp.zeros(dst.shape, dst.dtype)
-
     def drain(stage, plan):
         for d, (src, dst) in enumerate(plan):
 
@@ -184,6 +180,15 @@
     plan3 = side_plan((su3, rd3), (sd3, ru3), se3, hs3)
     plan4 = side_plan((d2.at[pl.ds(2, 2)], d2.at[pl.ds(10, 2)]), (d2.at[pl.ds(8, 2)], d2.at[pl.ds(0, 2)]), se4, hs4)
     plan5 = side_plan((d1.at[0], rd5), (d1.at[15], ru5), se5, hs5)
+
+    def blank(plans):
+        for d in range(8):
+
+            @pl.when(jnp.logical_not(exists(*DIRS[OPP[d]])))
+            def _():
+                for plan in plans:
+                    dst = plan[d][1]
+                    dst[...] = jnp.zeros(dst.shape, dst.dtype)
 
     lane8 = lanes((8, 128))
     for f in range(2):
@@ -305,6 +310,7 @@
         size = min(256, 1600 - at)
         w2t[:, at : at + size] = flip(one, w2n[at : at + size, :])
 
+    blank([plan0, *plan1, *plan2, plan3, plan4, plan5])
     arrive(0, plan0)
     for buf, at in ((ru0, 4), (rd0, 72)):
         tmp[...] = buf[...].astype(F32)
@@ -830,17 +836,16 @@
     drain(7, plan5)
 
 
-def to_pixels(planes, grad, want):
-    @pl.when(pl.program_id(0) == 0)
-    def _():
-        at = lax.broadcasted_iota(jnp.int32, (1024, 128), 0)
-        want[...] = 8 * (2 * (at % 64) + (at // 64) % 2) + at // 128 - lanes((1024, 128))
-
-    first = 256 * pl.program_id(0)
-    spread = jnp.concatenate(
-        [jnp.where(want[...] == first + 128 * j, 1.0, 0.0).astype(BF) for j in range(2)], axis=1
-    )
-    out = dot(planes[...], spread)
+def to_pixels(planes, grad):
+    at = lax.broadcasted_iota(jnp.int32, (128, 1024), 0)
+    want = 8 * (2 * (at % 64) + at // 64) - lanes((128, 1024))
+    out = None
+    for k in range(4):
+        spread = jnp.concatenate(
+            [jnp.where(want == -(2 * k + j), 1.0, 0.0).astype(BF) for j in range(2)], axis=0
+        )
+        part = dot(planes[:, 256 * k : 256 * k + 256], spread)
+        out = part if out is None else out + part
     for c in range(3):
         grad[c] = out[64 * c : 64 * c + 64] * (1.0 / SPREADS[c])
 
@@ -906,10 +911,8 @@
     grad = pl.pallas_call(
         to_pixels,
         out_shape=jax.ShapeDtypeStruct(image_gen.shape, F32),
-        grid=(4,),
-        in_specs=[pl.BlockSpec((192, 1024), lambda n: (0, 0))],
-        out_specs=pl.BlockSpec((3, 64, 256), lambda n: (0, 0, n)),
-        scratch_shapes=[pltpu.VMEM((1024, 128), jnp.int32)],
+        in_specs=[vmem],
+        out_specs=vmem,
         name="pixels",
     )(planes)
     return (grad, loss.reshape(()))

time: 53.3 us -> 52.3 us (0.981)
  Pallas kernels: 50.7 us -> 49.7 us
    pallas_call x1, Pallas kernels: 3.39 us -> 2.48 us  [local(): pl.pallas_call(to_pixels, out_shape=jax.ShapeDtypeStruct(image_gen.shape,...]
where the time goes in v4:
time: 52.3 us; the launch traced here: 52.1 us
  Pallas kernels  49.7 us (95%)
  between operations  2.4 us (5%)
    pallas_call x1, Pallas kernels, local(): pl.pallas_call(kernel, out_shape=(jax.ShapeDtypeStruct((192, 1024), BF),...  47.2 us
    pallas_call x1, Pallas kernels, local(): pl.pallas_call(to_pixels, out_shape=jax.ShapeDtypeStruct(image_gen.shape,...  2.48 us

profile of v4, /device:TPU:25, one launch (start us, length us, event | category | flops | bytes accessed | tf_op | source)
XLA Modules:
  0.0 52.1 jit_solution(11058959689482777448)
XLA Ops:
  0.6 47.2 %whole.1 = (bf16[192,1024]{1,0:T(8,128)(2,1)}, f32[1,1]{1,0:T(1,128)}) custom-call(f32[3,64,1024]{2,1,0:T(8,128)} %img0_hbm.1, f32[3,64,1024]{2,1,0:T(8,128)} %img1_hbm.1, bf16[432,64]{1,0:T(8,128)(2,1)} %bitcast.6, bf16[1600,192]{1,0:T(8,128)(2,1)} %bitcast.4, bf16[1728,96]{1,0:T(8,128)(2,1)} %bitcast.5, f32[64]{0:T(128)} %b1.1, f32[192]{0:T(256)} %b2.1, ...), custom_call_target="tpu_custom_call" | custom-call | tf_op jit(solution)/shard_map/whole/pallas_call | solution.py:894
  47.9 2.5 %pixels.1 = f32[3,64,1024]{2,1,0:T(8,128)} custom-call(bf16[192,1024]{1,0:T(8,128)(2,1)} %get-tuple-element.4.planes), custom_call_target="tpu_custom_call" | custom-call | tf_op jit(solution)/shard_map/pixels/pallas_call | solution.py:911

commit v5 on v4

--- a/solution.py
+++ b/solution.py
@@ -133,7 +133,8 @@
         )
 
     def start(stage, plan):
-        for d, (src, dst) in enumerate(plan):
+        for d in (UL, UR, DL, DR, LEFT, RIGHT, UP, DOWN):
+            src, dst = plan[d]
 
             @pl.when(exists(*DIRS[d]))
             def _():

time: 52.3 us -> 52.3 us (level)
  no operation moved by 1% of the time
where the time goes in v5:
time: 52.3 us; the launch traced here: 52.1 us
  Pallas kernels  49.7 us (95%)
  between operations  2.4 us (5%)
    pallas_call x1, Pallas kernels, local(): pl.pallas_call(kernel, out_shape=(jax.ShapeDtypeStruct((192, 1024), BF),...  47.2 us
    pallas_call x1, Pallas kernels, local(): pl.pallas_call(to_pixels, out_shape=jax.ShapeDtypeStruct(image_gen.shape,...  2.48 us

profile of v5, /device:TPU:25, one launch (start us, length us, event | category | flops | bytes accessed | tf_op | source)
XLA Modules:
  0.0 52.1 jit_solution(18018978433702596684)
XLA Ops:
  0.6 47.2 %whole.1 = (bf16[192,1024]{1,0:T(8,128)(2,1)}, f32[1,1]{1,0:T(1,128)}) custom-call(f32[3,64,1024]{2,1,0:T(8,128)} %img0_hbm.1, f32[3,64,1024]{2,1,0:T(8,128)} %img1_hbm.1, bf16[432,64]{1,0:T(8,128)(2,1)} %bitcast.6, bf16[1600,192]{1,0:T(8,128)(2,1)} %bitcast.4, bf16[1728,96]{1,0:T(8,128)(2,1)} %bitcast.5, f32[64]{0:T(128)} %b1.1, f32[192]{0:T(256)} %b2.1, ...), custom_call_target="tpu_custom_call" | custom-call | tf_op jit(solution)/shard_map/whole/pallas_call | solution.py:895
  47.9 2.5 %pixels.1 = f32[3,64,1024]{2,1,0:T(8,128)} custom-call(bf16[192,1024]{1,0:T(8,128)(2,1)} %get-tuple-element.4.planes), custom_call_target="tpu_custom_call" | custom-call | tf_op jit(solution)/shard_map/pixels/pallas_call | solution.py:912
